TPU v7x, 128 devices: a whole 4x4x4 slice. The times are simulated.
128 devices in a mesh: inb: 16 (over x, y), outb: 8 (over z, core).
Axes of the slice: x: 4, y: 4, z: 4, core: 2. Of those that a mesh axis runs over, the one named last changes fastest.
Arguments:
- tokens: bfloat16 [1024, 12288], P('outb', 'inb'), may hold values from -6 to 6
- weight_blocks: bfloat16 [16, 8, 72, 128, 128], P('inb', 'outb'), may hold values from -0.15625 to 0.15625
- block_rows: int32 [16, 8, 72], P('inb', 'outb'), may hold values from 0 to 95, as said below
- block_cols: int32 [16, 8, 72], P('inb', 'outb'), may hold values from 0 to 383, as said below
- block_count: int32 [16, 8], P('inb', 'outb'), may hold values from 9 to 72, as said below
- grad_act: bfloat16 [1024, 49152], P('inb', 'outb'), may hold values from -6 to 6
Outputs:
- activation: bfloat16 [1024, 49152], P('inb', 'outb')
- grad_tokens: float32 [1024, 12288], P('outb', 'inb')
- grad_weights: float32 [16, 8, 72, 128, 128], P('inb', 'outb')
Inputs may be any that keep to these rules, and one draw needn't show every extreme that they name: block_rows[a, b, s] lies in owner a's input blocks and block_cols[a, b, s] in owner b's hidden blocks; the slots of one owner name distinct blocks, dead slots included. `block_cols`: see block_rows. `block_count`: at least one owner has all 72 slots live.
All inputs are finite; a program needn't handle non-finite values.
Results may differ from a plain program's by a relative error of at most 0.02.
Values may be sent and summed in bfloat16 or wider, within the bound.
A program may use at most 192 MiB of HBM per device.

v0:
```python
import jax
import jax.numpy as jnp
from jax import lax
from jax.sharding import PartitionSpec as P

inv_root_two = 0.7071067811865476
inv_root_tau = 0.3989422804014327


def gelu_slope(values):
    normal_cdf = 0.5 * (1.0 + jax.scipy.special.erf(values * inv_root_two))
    return normal_cdf + values * jnp.exp(-0.5 * values * values) * inv_root_tau


def per_device(tokens, weight_blocks, block_rows, block_cols, block_count, grad_act):
    block_size = weight_blocks.shape[-1]
    capacity = weight_blocks.shape[2]
    gathered = lax.all_gather(tokens, "outb", axis=0, tiled=True)
    token_count = gathered.shape[0]
    row_blocks = gathered.shape[1] // block_size
    column_block_list = grad_act.shape[1] // block_size
    weights = weight_blocks[0, 0]
    row_local = block_rows[0, 0] - lax.axis_index("inb") * row_blocks
    col_local = block_cols[0, 0] - lax.axis_index("outb") * column_block_list
    is_live = jnp.arange(capacity, dtype=jnp.int32) < block_count[0, 0]
    input_blocks = jnp.take(
        gathered.reshape(token_count, row_blocks, block_size), row_local, axis=1
    )
    products = jnp.einsum(
        "tcf,cfh->tch", input_blocks, weights, preferred_element_type=jnp.float32
    ).astype(jnp.bfloat16)
    placing = (
        (col_local[:, None] == jnp.arange(column_block_list, dtype=jnp.int32)[None, :])
        & is_live[:, None]
    ).astype(jnp.bfloat16)
    partial_value = jnp.einsum(
        "tch,cj->tjh", products, placing, preferred_element_type=jnp.float32
    ).reshape(token_count, column_block_list * block_size)
    preact = lax.psum_scatter(
        partial_value.astype(jnp.bfloat16), "inb", scatter_dimension=0, tiled=True
    ).astype(jnp.float32)
    activation = jax.nn.gelu(preact, approximate=False).astype(jnp.bfloat16)
    grad_local = (grad_act.astype(jnp.float32) * gelu_slope(preact)).astype(jnp.bfloat16)
    grad_pre = lax.all_gather(grad_local, "inb", axis=0, tiled=True)
    row_onehot = (row_local[:, None] == jnp.arange(row_blocks, dtype=jnp.int32)[None, :]).astype(
        jnp.bfloat16
    )
    dense_weight = jnp.einsum(
        "cfh,cr,cj->rfjh", weights, row_onehot, placing, preferred_element_type=jnp.float32
    )
    dense_weight = dense_weight.astype(jnp.bfloat16).reshape(
        row_blocks * block_size, column_block_list * block_size
    )
    input_terms = jnp.einsum(
        "th,fh->tf", grad_pre, dense_weight, preferred_element_type=jnp.float32
    )
    grad_tokens = lax.psum_scatter(
        input_terms.astype(jnp.bfloat16), "outb", scatter_dimension=0, tiled=True
    ).astype(jnp.float32)
    grad_blocks = jnp.take(
        grad_pre.reshape(token_count, column_block_list, block_size), col_local, axis=1
    )
    grad_weights = jnp.einsum(
        "tcf,tch->cfh", input_blocks, grad_blocks, preferred_element_type=jnp.float32
    )
    grad_weights = grad_weights * is_live[:, None, None].astype(jnp.float32)
    return (activation, grad_tokens, grad_weights[None, None])


def solution(mesh):
    in_specs = (
        P("outb", "inb"),
        P("inb", "outb", None, None, None),
        P("inb", "outb", None),
        P("inb", "outb", None),
        P("inb", "outb"),
        P("inb", "outb"),
    )
    out_specs = (P("inb", "outb"), P("outb", "inb"), P("inb", "outb", None, None, None))
    return jax.shard_map(
        per_device, mesh=mesh, in_specs=in_specs, out_specs=out_specs, check_vma=False
    )
```

profile of v0, /device:TPU:0, one launch (start us, length us, event | category | flops | bytes accessed | tf_op | source)
XLA Modules:
  0.0 414.5 jit_solution(15111923576596091935)
XLA Ops:
  7.2 0.0 all-gather.3.cloned.1.call-start
  7.2 1.7 copy.24
  9.0 0.0 all-gather.3.cloned.1.call-update
  9.0 0.0 reduce-scatter.7.cloned.1.call-start
  9.7 0.7 fusion.76
  10.4 0.7 compare_and_fusion
  11.0 26.8 %all-gather.3.cloned.1.call-done = bf16[1024,768]{0,1:T(8,128)(2,1)} async-done(((bf16[128,768]{0,1:T(8,128)(2,1)}), bf16[1024,768]{0,1:T(8,128)(2,1)}) %all-gather.3.cloned.1.call-update) | async-done | bytes 1572880 | tf_op jit(solution)/shard_map/all_gather | solution.py:18
  37.9 1.9 copy.25
  39.8 8.3 %gather_fusion = bf16[72,1024,128]{2,1,0:T(8,128)(2,1)} fusion(bf16[1024,6,128]{2,0,1:T(8,128)(2,1)S(1)} %copy.25, s32[1024]{0:T(1024)S(1)} %pad_clamp_fusion.1), kind=kCustom, calls=%fused_computation | custom fusion | bytes 37749024 | tf_op jit(solution)/shard_map/jit(_take)/gather | solution.py:26
  48.1 19.6 %convert_bitcast_fusion = bf16[1024,72,128]{2,0,1:T(8,128)(2,1)} fusion(bf16[72,1024,128]{2,1,0:T(8,128)(2,1)} %gather_fusion, pred[72]{0:T(512)(128)(4,1)S(1)} %get-tuple-element.15, bf16[1,1,72,128,128]{4,3,2,1,0:T(8,128)(2,1)} %param.7), kind=kOutput, calls=%fused_computation.10 | convolution fusion | flops 2434793472 | bytes 40108104 | tf_op jit(solution)/shard_map/tcf,cfh->tch/dot_general | solution.py:29
  67.8 24.8 %convert_bitcast_fusion.1 = bf16[1024,48,128]{2,1,0:T(8,128)(2,1)} fusion(bf16[1024,72,128]{2,0,1:T(8,128)(2,1)} %convert_bitcast_fusion, s32[72]{0:T(128)S(1)} %get-tuple-element.10, pred[72]{0:T(512)(128)(4,1)S(1)} %iota_compare_fusion.2), kind=kOutput, calls=%fused_computation.13 | convolution fusion | flops 912268032 | bytes 31457640 | tf_op jit(solution)/shard_map/tch,cj->tjh/dot_general | solution.py:36
  92.5 16.9 %copy.37 = bf16[1024,48,128]{0,2,1:T(8,128)(2,1)} copy(bf16[1024,48,128]{2,1,0:T(8,128)(2,1)} %convert_bitcast_fusion.1) | data formatting | bytes 25165824 | tf_op jit(solution)/shard_map/convert_element_type | solution.py:40
  109.5 16.8 %copy.38 = bf16[1024,6144]{1,0:T(8,128)(2,1)} copy(bf16[1024,6144]{0,1:T(8,128)(2,1)} %bitcast.64) | data formatting | bytes 25165824
  126.2 0.0 copy-start
  126.2 0.0 reduce-scatter.7.cloned.1.call-update
  126.3 0.0 all-gather.5.cloned.1.call-start
  126.3 1.1 copy-done
  127.4 0.8 copy.28
  128.2 93.8 %reduce-scatter.7.cloned.1.call-done = bf16[64,6144]{1,0:T(8,128)(2,1)} async-done(((bf16[1024,6144]{1,0:T(8,128)(2,1)}), bf16[64,6144]{1,0:T(8,128)(2,1)}) %reduce-scatter.7.cloned.1.call-update) | async-done | bytes 786448
  222.1 2.4 copy.39
  224.5 10.0 %fusion.55 = (bf16[64,6144]{0,1:T(8,128)(2,1)}, bf16[64,6144]{0,1:T(8,128)(2,1)S(1)}) fusion(bf16[64,6144]{0,1:T(8,128)(2,1)} %copy.39, bf16[64,6144]{0,1:T(8,128)(2,1)S(1)} %copy.28), kind=kLoop, calls=%fused_computation.65 | loop fusion | flops 30277632 | bytes 3145728 | tf_op jit(solution)/shard_map/convert_element_type | solution.py:43
  234.6 2.4 copy.29
  237.0 0.0 all-gather.5.cloned.1.call-update
  237.0 0.0 reduce-scatter.5.cloned.1.call-start
  237.1 9.3 %convolution_convert_fusion = bf16[48,6,128,128]{3,0,2,1:T(8,128)(2,1)} fusion(bf16[72,128,128]{2,1,0:T(8,128)(2,1)} %bitcast.67, f32[72,6]{0,1:T(8,128)S(1)} %fusion.75, f32[72,48]{0,1:T(8,128)S(1)} %fusion.70), kind=kOutput, calls=%fused_computation.24 | convolution fusion | flops 684216576 | bytes 11812032 | tf_op jit(solution)/shard_map/cfh,cr,cj->rfjh/dot_general | solution.py:48
  246.4 79.5 %all-gather.5.cloned.1.call-done = bf16[1024,6144]{1,0:T(8,128)(2,1)} async-done(((bf16[64,6144]{1,0:T(8,128)(2,1)}), bf16[1024,6144]{1,0:T(8,128)(2,1)}) %all-gather.5.cloned.1.call-update) | async-done | bytes 12582928 | tf_op jit(solution)/shard_map/all_gather | solution.py:44
  325.8 0.0 copy-start.1
  325.8 15.9 %fusion.62 = bf16[1024,768]{1,0:T(8,128)(2,1)} fusion(bf16[1024,6144]{1,0:T(8,128)(2,1)} %all-gather.5.cloned.1.call-done, bf16[96,8,48,128]{3,2,1,0:T(8,128)(2,1)} %bitcast.66), kind=kOutput, calls=%fused_computation.68 | convolution fusion | flops 9664462848 | bytes 23592960 | tf_op jit(solution)/shard_map/th,fh->tf/dot_general | solution.py:54
  341.8 0.0 reduce-scatter.5.cloned.1.call-update
  341.8 0.0 copy-done.1
  341.8 1.4 copy.34
  343.2 16.5 %copy.31 = bf16[1024,6144]{0,1:T(8,128)(2,1)} copy(bf16[1024,6144]{1,0:T(8,128)(2,1)} %all-gather.5.cloned.1.call-done) | data formatting | bytes 25165824 | tf_op jit(solution)/shard_map/all_gather | solution.py:44
  359.8 16.7 %copy.32 = bf16[1024,48,128]{2,0,1:T(8,128)(2,1)} copy(bf16[1024,48,128]{0,2,1:T(8,128)(2,1)} %bitcast.65) | data formatting | bytes 25165824 | tf_op jit(solution)/shard_map/reshape | solution.py:61
  376.4 13.1 %gather_fusion.1 = bf16[72,1024,128]{2,1,0:T(8,128)(2,1)} fusion(bf16[1024,48,128]{2,0,1:T(8,128)(2,1)} %copy.32, s32[1024]{0:T(1024)S(1)} %pad_clamp_fusion), kind=kCustom, calls=%fused_computation.1 | custom fusion | bytes 37749024 | tf_op jit(solution)/shard_map/jit(_take)/gather | solution.py:60
  389.5 16.7 %multiply_bitcast_fusion = f32[1,1,72,128,128]{4,3,2,1,0:T(8,128)} fusion(f32[72]{0:T(128)S(1)} %fusion.81, bf16[72,1024,128]{2,1,0:T(8,128)(2,1)} %gather_fusion.1, pred[72]{0:T(512)(128)(4,1)S(1)} %get-tuple-element.9, bf16[72,1024,128]{2,1,0:T(8,128)(2,1)} %gather_fusion, pred[72]{0:T(512)(128)(4,1)S(1)} %get-tuple-element.15), kind=kOutput, calls=%fused_computation.26 | convolution fusion | flops 2435973120 | bytes 42467760 | tf_op jit(solution)/shard_map/tcf,tch->cfh/dot_general | solution.py:63
  406.2 0.0 reduce-scatter.5.cloned.1.call-done
  406.2 1.7 convert_element_type.61
  (7 shorter events, 0.0 us)
Async XLA Ops:
  7.2 30.7 %all-gather.3.cloned.1.call-start = ((), (), s32[]{:S(2)}) async-start(), calls=%async_computation.2 | async-start | bytes 1769472 | tf_op jit(solution)/shard_map/all_gather | solution.py:18
  9.0 213.1 %reduce-scatter.7.cloned.1.call-start = ((), (), s32[]{:S(2)}) async-start(), calls=%async_computation.5 | async-start | bytes 13369344
  126.2 1.1 copy-start
  126.3 199.6 %all-gather.5.cloned.1.call-start = ((), (), s32[]{:S(2)}) async-start(), calls=%async_computation.3 | async-start | bytes 13369344 | tf_op jit(solution)/shard_map/all_gather | solution.py:44
  237.0 169.2 %reduce-scatter.5.cloned.1.call-start = ((), (), s32[]{:S(2)}) async-start(), calls=%async_computation.4 | async-start | bytes 1769472 | tf_op jit(solution)/shard_map/reduce_scatter | solution.py:57
  325.8 16.0 %copy-start.1 = (s32[1,1,72]{2,1,0:T(1,128)S(1)}, s32[1,1,72]{2,1,0:T(1,128)}, u32[]{:S(2)}) copy-start(s32[1,1,72]{2,1,0:T(1,128)} %param.9) | copy-start | bytes 868
Sparse Core Ops, SparseCore 0:
  10.2 27.6 all-gather.2
  126.4 95.6 reduce-scatter.6
  237.1 88.6 all-gather.4
  341.9 32.9 reduce-scatter.4
where the time goes:
time: 417 us; the launch traced here: 414 us
  waiting for transfers between devices  200 us (48%)
  local copies, waits for them, and re-layouts  100 us (24%)
  matrix products  86.4 us (21%)
  between operations  14.5 us (3%)
  other arithmetic  13.1 us (3%)
    unnamed x5, waiting for transfers between devices  93.9 us
    all_gather x1, waiting for transfers between devices, per_device(): grad_pre = lax.all_gather(grad_local, 'inb', axis=0, tiled=True)  79.5 us
    all_gather x1, waiting for transfers between devices, per_device(): gathered = lax.all_gather(tokens, 'outb', axis=0, tiled=True)  26.8 us
    dot_general x1, matrix products, per_device(): jnp.einsum('tch,cj->tjh', products, placing, preferred_element_type=jnp.f...  24.8 us
    unnamed x9, local copies, waits for them, and re-layouts  24.3 us
    dot_general x1, matrix products, per_device(): jnp.einsum('tcf,cfh->tch', input_blocks, weights, preferred_element_type=...  19.6 us
    convert_element_type x1, local copies, waits for them, and re-layouts, per_device(): partial_value.astype(jnp.bfloat16)  16.9 us
    dot_general x1, matrix products, per_device(): jnp.einsum('tcf,tch->cfh', input_blocks, grad_blocks, preferred_element_t...  16.7 us
  transfers between devices with their start and end apart: 4, of which 3 were waited for; matrix products, arithmetic and copies ran while one was open for 18% of the time, Pallas kernels for 0%

commit v1 on v0

v1 whole, which is shorter than its diff:
```python
import functools

import jax
import jax.numpy as jnp
from jax import lax
from jax.experimental import pallas as pl
from jax.experimental.pallas import tpu as pltpu
from jax.sharding import PartitionSpec as P

MESH = pl.DeviceIdType.MESH
F32 = jnp.float32
BF16 = jnp.bfloat16
INV_ROOT_TWO = 0.7071067811865476
INV_ROOT_TAU = 0.3989422804014327
BLK = 128
RB = 6
CBK = 48
CAP = 72
WB = 2
W = WB * BLK
NCH = CBK // (2 * WB)
SL = 4


def add2(a, b):
    return (a.astype(F32) + b.astype(F32)).astype(BF16)


def kernel(
    idx, cell, live, tok, wblk, gact,
    act, dx_out, gw_out,
    wp, xs, xt, ps, r1, r2, qs, t1, t2, gs, dxa, gw, sb, sr, eb, u1, u2,
    ssem, rsem, asem, arsem, lsem,
):
    a = lax.axis_index("inb")
    b = lax.axis_index("outb")
    x, y = a // 4, a % 4
    z, c = b // 2, b % 2

    def up(v):
        return lax.rem(v + 1, 4)

    def down(v):
        return lax.rem(v + 3, 4)

    def opp(v):
        return lax.rem(v + 2, 4)

    zr, zl, zo = up(z), down(z), opp(z)
    sib = (a, 2 * z + (1 - c))
    zr_dev, zl_dev = (a, 2 * zr + c), (a, 2 * zl + c)

    first = (x, y)
    second = (y, x)

    def dev_first(t, v):
        return (4 * v + y, b) if t == 0 else (4 * x + v, b)

    def dev_second(t, v):
        return (4 * x + v, b) if t == 0 else (4 * v + y, b)

    wcopy = pltpu.make_async_copy(wblk, wp.at[pl.ds(0, CAP)], lsem.at[0])
    wcopy.start()
    xcopy = pltpu.make_async_copy(tok, xs.at[b], lsem.at[1])
    xcopy.start()

    barrier = pltpu.get_barrier_semaphore()
    for dev in (
        dev_first(0, up(x)), dev_first(0, down(x)),
        dev_first(1, up(y)), dev_first(1, down(y)),
        zr_dev, zl_dev, sib,
    ):
        pl.semaphore_signal(barrier, inc=1, device_id=dev, device_id_type=MESH)
    wp[CAP] = jnp.zeros((BLK, BLK), BF16)
    pl.semaphore_wait(barrier, 7)

    def ac(n, src, dst, dev):
        return pltpu.make_async_remote_copy(
            src_ref=src, dst_ref=dst, send_sem=asem.at[n], recv_sem=arsem.at[n],
            device_id=dev, device_id_type=MESH,
        )

    def xb(zz, cc):
        return xs.at[2 * zz + cc]

    def xh(zz, cc, h):
        return xs.at[2 * zz + cc, pl.ds(64 * h, 64)]

    sends = []

    def go(n, src, dst, dev):
        d = ac(n, src, dst, dev)
        d.start()
        sends.append(d)

    def got(n, dst):
        ac(n, dst, dst, sib).wait_recv()

    go(0, tok, xb(z, c), zr_dev)
    go(1, tok, xb(z, c), zl_dev)
    go(2, tok, xb(z, c), sib)
    got(0, xb(zl, c))
    go(3, xh(zl, c, 0), xh(zl, c, 0), zr_dev)
    got(1, xb(zr, c))
    go(4, xh(zr, c, 1), xh(zr, c, 1), zl_dev)
    go(5, xb(zl, c), xb(zl, c), sib)
    go(6, xb(zr, c), xb(zr, c), sib)
    got(3, xh(zo, c, 0))
    go(7, xh(zo, c, 0), xh(zo, c, 0), sib)
    got(4, xh(zo, c, 1))
    go(8, xh(zo, c, 1), xh(zo, c, 1), sib)
    xcopy.wait()
    wcopy.wait()
    got(2, xb(z, 1 - c))
    got(5, xb(zl, 1 - c))
    got(6, xb(zr, 1 - c))
    got(7, xh(zo, 1 - c, 0))
    got(8, xh(zo, 1 - c, 1))
    for d in sends:
        d.wait_send()

    dxa[...] = jnp.zeros_like(dxa)
    for r in range(RB):
        for q in range(8):
            xt[r * BLK:(r + 1) * BLK, q * BLK:(q + 1) * BLK] = xs[q, :, r * BLK:(r + 1) * BLK].T

    def weights(k):
        cols = []
        for j in range(2 * WB):
            col = 2 * WB * k + j
            cols.append(jnp.concatenate([wp[idx[r * CBK + col]] for r in range(RB)], axis=0))
        return jnp.concatenate(cols, axis=1)

    def copy(k, t, n, src, dst, dev):
        slot = lax.rem(k, SL)
        return pltpu.make_async_remote_copy(
            src_ref=src, dst_ref=dst,
            send_sem=ssem.at[slot, t, n], recv_sem=rsem.at[slot, t, n],
            device_id=dev, device_id_type=MESH,
        )

    def start(k, t, n, src, dst, dev):
        copy(k, t, n, src, dst, dev).start()

    def arrived(k, t, n, dst):
        copy(k, t, n, dst, dst, sib).wait_recv()

    def sent(k, t, n, src):
        copy(k, t, n, src, src, sib).wait_send()

    def stage0(k):
        slot = lax.rem(k, SL)
        rhs = weights(k)
        for m in range(4):
            lhs = jnp.concatenate([xs[2 * m], xs[2 * m + 1]], axis=0)
            out = jnp.dot(lhs, rhs, preferred_element_type=F32).astype(BF16)
            for n in range(4):
                ps[slot, 0, m, n] = out[64 * n:64 * n + 64, :W]
                ps[slot, 1, n, m] = out[64 * n:64 * n + 64, W:]
        for t in range(2):
            f = first[t]
            r, l, o = up(f), down(f), opp(f)
            lo, hi = pl.ds(0, 2), pl.ds(2, 2)
            start(k, t, 0, ps.at[slot, t, o, lo], r1.at[slot, t, 0], dev_first(t, r))
            start(k, t, 1, ps.at[slot, t, o, hi], r1.at[slot, t, 1], dev_first(t, l))
            start(k, t, 2, ps.at[slot, t, r, hi], r2.at[slot, t, 0, hi], dev_first(t, r))
            start(k, t, 3, ps.at[slot, t, l, lo], r2.at[slot, t, 1, lo], dev_first(t, l))

    def stage1(k):
        slot = lax.rem(k, SL)
        for t in range(2):
            f = first[t]
            r, l = up(f), down(f)
            lo, hi = pl.ds(0, 2), pl.ds(2, 2)
            arrived(k, t, 0, r1.at[slot, t, 0])
            ps[slot, t, r, lo] = add2(ps[slot, t, r, lo], r1[slot, t, 0])
            start(k, t, 4, ps.at[slot, t, r, lo], r2.at[slot, t, 0, lo], dev_first(t, r))
            arrived(k, t, 1, r1.at[slot, t, 1])
            ps[slot, t, l, hi] = add2(ps[slot, t, l, hi], r1[slot, t, 1])
            start(k, t, 5, ps.at[slot, t, l, hi], r2.at[slot, t, 1, hi], dev_first(t, l))

    def stage2(k):
        slot = lax.rem(k, SL)
        for t in range(2):
            f, s = first[t], second[t]
            lo, hi = pl.ds(0, 2), pl.ds(2, 2)
            arrived(k, t, 2, r2.at[slot, t, 0, hi])
            arrived(k, t, 3, r2.at[slot, t, 1, lo])
            arrived(k, t, 4, r2.at[slot, t, 0, lo])
            arrived(k, t, 5, r2.at[slot, t, 1, hi])
            qs[slot, t] = (
                ps[slot, t, f].astype(F32) + r2[slot, t, 0].astype(F32) + r2[slot, t, 1].astype(F32)
            ).astype(BF16)
            for n in range(6):
                sent(k, t, n, r1.at[slot, t, 0])
            r, l, o = up(s), down(s), opp(s)
            lo, hi = pl.ds(0, 32), pl.ds(32, 32)
            start(k, t, 6, qs.at[slot, t, o, lo], t1.at[slot, t, 0], dev_second(t, r))
            start(k, t, 7, qs.at[slot, t, o, hi], t1.at[slot, t, 1], dev_second(t, l))
            start(k, t, 8, qs.at[slot, t, r, hi], t2.at[slot, t, 0, hi], dev_second(t, r))
            start(k, t, 9, qs.at[slot, t, l, lo], t2.at[slot, t, 1, lo], dev_second(t, l))

    def stage3(k):
        slot = lax.rem(k, SL)
        for t in range(2):
            s = second[t]
            r, l = up(s), down(s)
            lo, hi = pl.ds(0, 32), pl.ds(32, 32)
            arrived(k, t, 6, t1.at[slot, t, 0])
            qs[slot, t, r, lo] = add2(qs[slot, t, r, lo], t1[slot, t, 0])
            start(k, t, 10, qs.at[slot, t, r, lo], t2.at[slot, t, 0, lo], dev_second(t, r))
            arrived(k, t, 7, t1.at[slot, t, 1])
            qs[slot, t, l, hi] = add2(qs[slot, t, l, hi], t1[slot, t, 1])
            start(k, t, 11, qs.at[slot, t, l, hi], t2.at[slot, t, 1, hi], dev_second(t, l))

    def stage4(k):
        slot = lax.rem(k, SL)
        for t in range(2):
            f, s = first[t], second[t]
            lo, hi = pl.ds(0, 32), pl.ds(32, 32)
            arrived(k, t, 8, t2.at[slot, t, 0, hi])
            arrived(k, t, 9, t2.at[slot, t, 1, lo])
            arrived(k, t, 10, t2.at[slot, t, 0, lo])
            arrived(k, t, 11, t2.at[slot, t, 1, hi])
            pre = qs[slot, t, s].astype(F32) + t2[slot, t, 0].astype(F32) + t2[slot, t, 1].astype(F32)
            cdf = 0.5 * (1.0 + lax.erf(pre * INV_ROOT_TWO))
            cols = pl.ds(pl.multiple_of((2 * k + t) * W, W), W)
            act[:, cols] = (pre * cdf).astype(BF16)
            slope = cdf + pre * jnp.exp(-0.5 * pre * pre) * INV_ROOT_TAU
            gs[k, t, f, s] = (gact[:, cols].astype(F32) * slope).astype(BF16)
            for n in range(6, 12):
                sent(k, t, n, t1.at[slot, t, 0])
            start(k, t, 12, gs.at[k, t, f, s], gs.at[k, t, f, s], dev_second(t, up(s)))
            start(k, t, 13, gs.at[k, t, f, s], gs.at[k, t, f, s], dev_second(t, down(s)))

    def stage5(k):
        for t in range(2):
            f, s = first[t], second[t]
            r, l = up(s), down(s)
            lo, hi = pl.ds(0, 32), pl.ds(32, 32)
            arrived(k, t, 12, gs.at[k, t, f, l])
            start(k, t, 14, gs.at[k, t, f, l, lo], gs.at[k, t, f, l, lo], dev_second(t, r))
            arrived(k, t, 13, gs.at[k, t, f, r])
            start(k, t, 15, gs.at[k, t, f, r, hi], gs.at[k, t, f, r, hi], dev_second(t, l))

    def stage6(k):
        for t in range(2):
            f, s = first[t], second[t]
            o = opp(s)
            lo, hi = pl.ds(0, 32), pl.ds(32, 32)
            arrived(k, t, 14, gs.at[k, t, f, o, lo])
            arrived(k, t, 15, gs.at[k, t, f, o, hi])
            start(k, t, 16, gs.at[k, t, f], gs.at[k, t, f], dev_first(t, up(f)))
            start(k, t, 17, gs.at[k, t, f], gs.at[k, t, f], dev_first(t, down(f)))

    def stage7(k):
        for t in range(2):
            f = first[t]
            r, l = up(f), down(f)
            lo, hi = pl.ds(0, 2), pl.ds(2, 2)
            arrived(k, t, 16, gs.at[k, t, l])
            start(k, t, 18, gs.at[k, t, l, lo], gs.at[k, t, l, lo], dev_first(t, r))
            arrived(k, t, 17, gs.at[k, t, r])
            start(k, t, 19, gs.at[k, t, r, hi], gs.at[k, t, r, hi], dev_first(t, l))

    def stage8(k):
        for t in range(2):
            f, s = first[t], second[t]
            o = opp(f)
            lo, hi = pl.ds(0, 2), pl.ds(2, 2)
            arrived(k, t, 18, gs.at[k, t, o, lo])
            arrived(k, t, 19, gs.at[k, t, o, hi])
            sent(k, t, 12, gs.at[k, t, f, s])
            sent(k, t, 13, gs.at[k, t, f, s])
            sent(k, t, 14, gs.at[k, t, f, s, pl.ds(0, 32)])
            sent(k, t, 15, gs.at[k, t, f, s, pl.ds(0, 32)])
            sent(k, t, 16, gs.at[k, t, f])
            sent(k, t, 17, gs.at[k, t, f])
            sent(k, t, 18, gs.at[k, t, o, lo])
            sent(k, t, 19, gs.at[k, t, o, hi])
        rhs = weights(k)
        g0 = jnp.concatenate([gs[k, 0, n // 4, n % 4] for n in range(16)], axis=0)
        g1 = jnp.concatenate([gs[k, 1, n % 4, n // 4] for n in range(16)], axis=0)
        g = jnp.concatenate([g0, g1], axis=1)
        term = lax.dot_general(g, rhs, (((1,), (1,)), ((), ())), preferred_element_type=F32)
        dxa[...] += term.reshape(8, BLK, RB * BLK)
        wg = jnp.dot(xt[...], g, preferred_element_type=F32)
        for r in range(RB):
            for j in range(2 * WB):
                gw[r * CBK + 2 * WB * k + j] = wg[r * BLK:(r + 1) * BLK, j * BLK:(j + 1) * BLK]

    stages = (stage0, stage1, stage2, stage3, stage4, stage5, stage6, stage7, stage8)

    def body(i, carry):
        for n in range(len(stages) - 1, -1, -1):
            k = i - n

            @pl.when((k >= 0) & (k < NCH))
            def _():
                stages[n](k)

        return carry

    lax.fori_loop(0, NCH + len(stages) - 1, body, 0)

    sends.clear()
    for q in range(4):
        sb[q] = dxa[2 * q + (1 - c)].astype(BF16)
    go(9, sb, sr, sib)

    def extract(s, carry):
        gw_out[s] = gw[cell[s]] * live[s]
        return carry

    got(9, sr)
    for q in range(4):
        eb[q] = (dxa[2 * q + c] + sr[q].astype(F32)).astype(BF16)
    lo, hi = pl.ds(0, 64), pl.ds(64, 64)
    go(10, eb.at[zo, lo], u1.at[0], zr_dev)
    go(11, eb.at[zo, hi], u1.at[1], zl_dev)
    go(12, eb.at[zr, hi], u2.at[0, hi], zr_dev)
    go(13, eb.at[zl, lo], u2.at[1, lo], zl_dev)
    lax.fori_loop(0, CAP // 2, extract, 0)
    got(10, u1.at[0])
    eb[zr, lo] = add2(eb[zr, lo], u1[0])
    go(14, eb.at[zr, lo], u2.at[0, lo], zr_dev)
    got(11, u1.at[1])
    eb[zl, hi] = add2(eb[zl, hi], u1[1])
    go(15, eb.at[zl, hi], u2.at[1, hi], zl_dev)
    lax.fori_loop(CAP // 2, CAP, extract, 0)
    got(12, u2.at[0, hi])
    got(13, u2.at[1, lo])
    got(14, u2.at[0, lo])
    got(15, u2.at[1, hi])
    dx_out[...] = eb[z].astype(F32) + u2[0].astype(F32) + u2[1].astype(F32)
    for d in sends:
        d.wait_send()


def per_device(tokens, weight_blocks, block_rows, block_cols, block_count, grad_act):
    slot_ids = jnp.arange(CAP, dtype=jnp.int32)
    row_local = block_rows[0, 0] - lax.axis_index("inb") * RB
    col_local = block_cols[0, 0] - lax.axis_index("outb") * CBK
    is_live = slot_ids < block_count[0, 0]
    cell = row_local * CBK + col_local
    hit = (jnp.arange(RB * CBK, dtype=jnp.int32)[:, None] == cell[None, :]) & is_live[None, :]
    idx = CAP - jnp.sum(jnp.where(hit, CAP - slot_ids[None, :], 0), axis=1)
    vmem = pl.BlockSpec(memory_space=pltpu.VMEM)
    smem = pl.BlockSpec(memory_space=pltpu.SMEM)
    out = pl.pallas_call(
        kernel,
        out_shape=(
            jax.ShapeDtypeStruct((64, CBK * BLK), BF16),
            jax.ShapeDtypeStruct((BLK, RB * BLK), F32),
            jax.ShapeDtypeStruct((CAP, BLK, BLK), F32),
        ),
        in_specs=[smem, smem, smem, vmem, pl.BlockSpec(memory_space=pl.ANY), vmem],
        out_specs=(vmem, vmem, vmem),
        scratch_shapes=[
            pltpu.VMEM((CAP + 1, BLK, BLK), BF16),
            pltpu.VMEM((8, BLK, RB * BLK), BF16),
            pltpu.VMEM((RB * BLK, 1024), BF16),
            pltpu.VMEM((SL, 2, 4, 4, 64, W), BF16),
            pltpu.VMEM((SL, 2, 2, 2, 64, W), BF16),
            pltpu.VMEM((SL, 2, 2, 4, 64, W), BF16),
            pltpu.VMEM((SL, 2, 4, 64, W), BF16),
            pltpu.VMEM((SL, 2, 2, 32, W), BF16),
            pltpu.VMEM((SL, 2, 2, 64, W), BF16),
            pltpu.VMEM((NCH, 2, 4, 4, 64, W), BF16),
            pltpu.VMEM((8, BLK, RB * BLK), F32),
            pltpu.VMEM((RB * CBK, BLK, BLK), F32),
            pltpu.VMEM((4, BLK, RB * BLK), BF16),
            pltpu.VMEM((4, BLK, RB * BLK), BF16),
            pltpu.VMEM((4, BLK, RB * BLK), BF16),
            pltpu.VMEM((2, 64, RB * BLK), BF16),
            pltpu.VMEM((2, BLK, RB * BLK), BF16),
            pltpu.SemaphoreType.DMA((SL, 2, 20)),
            pltpu.SemaphoreType.DMA((SL, 2, 20)),
            pltpu.SemaphoreType.DMA((16,)),
            pltpu.SemaphoreType.DMA((16,)),
            pltpu.SemaphoreType.DMA((2,)),
        ],
        compiler_params=pltpu.CompilerParams(
            collective_id=0, has_side_effects=True, vmem_limit_bytes=67043328
        ),
        name="ffn",
    )(idx, cell, is_live.astype(F32), tokens, weight_blocks[0, 0], grad_act)
    activation, grad_tokens, grad_weights = out
    return (activation, grad_tokens, grad_weights[None, None])


def solution(mesh):
    in_specs = (
        P("outb", "inb"),
        P("inb", "outb", None, None, None),
        P("inb", "outb", None),
        P("inb", "outb", None),
        P("inb", "outb"),
        P("inb", "outb"),
    )
    out_specs = (P("inb", "outb"), P("outb", "inb"), P("inb", "outb", None, None, None))
    return jax.shard_map(
        per_device, mesh=mesh, in_specs=in_specs, out_specs=out_specs, check_vma=False
    )
```

time: 417 us -> 188 us (0.45)
  waiting for transfers between devices: 200 us -> 0 us
  Pallas kernels: 0 us -> 174 us
  local copies, waits for them, and re-layouts: 100 us -> 8.92 us
  matrix products: 86.4 us -> 0 us
  between operations: 14.5 us -> 1.3 us
  other arithmetic: 13.1 us -> 1.89 us
    pallas_call x0 -> x1, Pallas kernels: none -> 174 us  [per_device(): pl.pallas_call(kernel, out_shape=(jax.ShapeDtypeStruct((64, CBK * BLK), B...]
    all_gather x2 -> x0, waiting for transfers between devices: 106 us -> none  [the longest x1 79.5 us: per_device(): grad_pre = lax.all_gather(grad_local, 'inb', axis=0, tiled=True)]
    unnamed x5 -> x0, waiting for transfers between devices: 93.9 us -> none
    dot_general x5 -> x0, matrix products: 86.4 us -> none  [the longest x1 24.8 us: per_device(): jnp.einsum('tch,cj->tjh', products, placing, preferred_element_type=jnp.f...]
    gather x2 -> x0, local copies, waits for them, and re-layouts: 21.4 us -> none  [the longest x1 13.1 us: per_device(): jnp.take(grad_pre.reshape(token_count, column_block_list, block_size), co...]
    convert_element_type x2 -> x0, local copies, waits for them, and re-layouts: 19.4 us -> none  [the longest x1 16.9 us: per_device(): partial_value.astype(jnp.bfloat16)]
    reshape x2 -> x0, local copies, waits for them, and re-layouts: 18.6 us -> none  [the longest x1 16.7 us: per_device(): grad_pre.reshape(token_count, column_block_list, block_size)]
    all_gather x1 -> x0, local copies, waits for them, and re-layouts: 16.5 us -> none  [per_device(): grad_pre = lax.all_gather(grad_local, 'inb', axis=0, tiled=True)]
  transfers between devices with their start and end apart: 4 -> 0, of which waited for: 3 -> 0; matrix products, arithmetic and copies ran while one was open for 18% -> 0% of each run, Pallas kernels for 0% -> 0%
where the time goes in v1:
time: 188 us; the launch traced here: 186 us
  Pallas kernels  174 us (93%)
  local copies, waits for them, and re-layouts  8.92 us (5%)
  other arithmetic  1.89 us (1%)
    pallas_call x1, Pallas kernels, per_device(): pl.pallas_call(kernel, out_shape=(jax.ShapeDtypeStruct((64, CBK * BLK), B...  174 us
    unnamed x5, local copies, waits for them, and re-layouts  8.92 us

profile of v1, /device:TPU:0, one launch (start us, length us, event | category | flops | bytes accessed | tf_op | source)
XLA Modules:
  0.0 185.8 jit_solution(14094190432561218860)
XLA Ops:
  1.3 0.7 add_bitcast_fusion.cell
  2.0 0.0 copy-start
  2.0 0.5 iota_compare_fusion.1
  2.5 0.0 copy-done
  2.5 0.1 select_reduce_fusion
  2.6 0.6 broadcast_subtract_fusion.idx
  3.2 173.7 %ffn.1 = (bf16[64,6144]{1,0:T(8,128)(2,1)}, f32[128,768]{1,0:T(8,128)}, f32[72,128,128]{2,1,0:T(8,128)}) custom-call(s32[288]{0:T(512)} %broadcast_subtract_fusion.idx, s32[72]{0:T(128)} %copy-done, f32[72]{0:T(128)} %get-tuple-element.10.live, bf16[128,768]{1,0:T(8,128)(2,1)} %tok.1, bf16[72,128,128]{2,1,0:T(8,128)(2,1)} %bitcast.7, bf16[64,6144]{1,0:T(8,128)(2,1)} %gact.1), custom_call_target="tpu_custom_call" | custom-call | tf_op jit(solution)/shard_map/ffn/pallas_call | solution.py:350
  176.9 2.1 %copy.13 = bf16[64,6144]{1,0:T(8,128)(2,1)} copy(bf16[64,6144]{1,0:T(8,128)(2,1)} %get-tuple-element.14) | data formatting | bytes 1572864
  179.0 1.8 copy.14
  180.7 5.1 %copy.15 = f32[1,1,72,128,128]{4,3,2,1,0:T(8,128)} copy(f32[1,1,72,128,128]{4,3,2,1,0:T(8,128)} %bitcast.6) | data formatting | bytes 9437184
  (1 shorter events, 0.0 us)
Async XLA Ops:
  2.0 0.5 copy-start

commit v2 on v1

--- a/solution.py
+++ b/solution.py
@@ -27,10 +27,10 @@
 
 
 def kernel(
-    idx, cell, live, tok, wblk, gact,
-    act, dx_out, gw_out,
-    wp, xs, xt, ps, r1, r2, qs, t1, t2, gs, dxa, gw, sb, sr, eb, u1, u2,
-    ssem, rsem, asem, arsem, lsem,
+    idx, tok, wblk, gact_hbm,
+    act_hbm, dx_out, gw_hbm,
+    wp, xs, xt, ps, r1, r2, qs, t1, t2, gs, dxa, gact, act, gwst, sb, sr, eb, u1, u2,
+    ssem, rsem, asem, arsem, lsem, osem, gsem,
 ):
     a = lax.axis_index("inb")
     b = lax.axis_index("outb")
@@ -63,6 +63,8 @@
     wcopy.start()
     xcopy = pltpu.make_async_copy(tok, xs.at[b], lsem.at[1])
     xcopy.start()
+    gcopy = pltpu.make_async_copy(gact_hbm, gact, lsem.at[2])
+    gcopy.start()
 
     barrier = pltpu.get_barrier_semaphore()
     for dev in (
@@ -96,33 +98,22 @@
     def got(n, dst):
         ac(n, dst, dst, sib).wait_recv()
 
-    go(0, tok, xb(z, c), zr_dev)
-    go(1, tok, xb(z, c), zl_dev)
-    go(2, tok, xb(z, c), sib)
-    got(0, xb(zl, c))
-    go(3, xh(zl, c, 0), xh(zl, c, 0), zr_dev)
-    got(1, xb(zr, c))
-    go(4, xh(zr, c, 1), xh(zr, c, 1), zl_dev)
-    go(5, xb(zl, c), xb(zl, c), sib)
-    go(6, xb(zr, c), xb(zr, c), sib)
-    got(3, xh(zo, c, 0))
-    go(7, xh(zo, c, 0), xh(zo, c, 0), sib)
-    got(4, xh(zo, c, 1))
-    go(8, xh(zo, c, 1), xh(zo, c, 1), sib)
+    th = [tok.at[pl.ds(0, 64)], tok.at[pl.ds(64, 64)]]
+    go(0, th[0], xh(z, c, 0), zr_dev)
+    go(1, th[1], xh(z, c, 1), zl_dev)
+    go(2, th[1], xh(z, c, 1), zr_dev)
+    go(3, th[0], xh(z, c, 0), zl_dev)
+    go(4, tok, xb(z, c), sib)
+    dxa[...] = jnp.zeros_like(dxa)
+    got(0, xh(zl, c, 0))
+    go(5, xh(zl, c, 0), xh(zl, c, 0), zr_dev)
+    got(1, xh(zr, c, 1))
+    go(6, xh(zr, c, 1), xh(zr, c, 1), zl_dev)
+    go(7, xh(zl, c, 0), xh(zl, c, 0), sib)
+    go(8, xh(zr, c, 1), xh(zr, c, 1), sib)
     xcopy.wait()
     wcopy.wait()
-    got(2, xb(z, 1 - c))
-    got(5, xb(zl, 1 - c))
-    got(6, xb(zr, 1 - c))
-    got(7, xh(zo, 1 - c, 0))
-    got(8, xh(zo, 1 - c, 1))
-    for d in sends:
-        d.wait_send()
-
-    dxa[...] = jnp.zeros_like(dxa)
-    for r in range(RB):
-        for q in range(8):
-            xt[r * BLK:(r + 1) * BLK, q * BLK:(q + 1) * BLK] = xs[q, :, r * BLK:(r + 1) * BLK].T
+    got(4, xb(z, 1 - c))
 
     def weights(k):
         cols = []
@@ -148,15 +139,21 @@
     def sent(k, t, n, src):
         copy(k, t, n, src, src, sib).wait_send()
 
+    def rows(slot, m, rhs):
+        lhs = jnp.concatenate([xs[2 * m], xs[2 * m + 1]], axis=0)
+        out = jnp.dot(lhs, rhs, preferred_element_type=F32).astype(BF16)
+        for n in range(4):
+            ps[slot, 0, m, n] = out[64 * n:64 * n + 64, :W]
+            ps[slot, 1, n, m] = out[64 * n:64 * n + 64, W:]
+
     def stage0(k):
-        slot = lax.rem(k, SL)
         rhs = weights(k)
         for m in range(4):
-            lhs = jnp.concatenate([xs[2 * m], xs[2 * m + 1]], axis=0)
-            out = jnp.dot(lhs, rhs, preferred_element_type=F32).astype(BF16)
-            for n in range(4):
-                ps[slot, 0, m, n] = out[64 * n:64 * n + 64, :W]
-                ps[slot, 1, n, m] = out[64 * n:64 * n + 64, W:]
+            rows(lax.rem(k, SL), m, rhs)
+        send0(k)
+
+    def send0(k):
+        slot = lax.rem(k, SL)
         for t in range(2):
             f = first[t]
             r, l, o = up(f), down(f), opp(f)
@@ -225,7 +222,12 @@
             pre = qs[slot, t, s].astype(F32) + t2[slot, t, 0].astype(F32) + t2[slot, t, 1].astype(F32)
             cdf = 0.5 * (1.0 + lax.erf(pre * INV_ROOT_TWO))
             cols = pl.ds(pl.multiple_of((2 * k + t) * W, W), W)
-            act[:, cols] = (pre * cdf).astype(BF16)
+            @pl.when(k >= SL)
+            def _():
+                pltpu.make_async_copy(act.at[slot, t], act_hbm.at[:, cols], osem.at[slot, t]).wait()
+
+            act[slot, t] = (pre * cdf).astype(BF16)
+            pltpu.make_async_copy(act.at[slot, t], act_hbm.at[:, cols], osem.at[slot, t]).start()
             slope = cdf + pre * jnp.exp(-0.5 * pre * pre) * INV_ROOT_TAU
             gs[k, t, f, s] = (gact[:, cols].astype(F32) * slope).astype(BF16)
             for n in range(6, 12):
@@ -263,7 +265,16 @@
             arrived(k, t, 17, gs.at[k, t, r])
             start(k, t, 19, gs.at[k, t, r, hi], gs.at[k, t, r, hi], dev_first(t, l))
 
-    def stage8(k):
+    def gw_copies(k):
+        g = lax.rem(k, 2)
+        return [
+            pltpu.make_async_copy(
+                gwst.at[g, r], gw_hbm.at[pl.ds(r * CBK + 2 * WB * k, 2 * WB)], gsem.at[g, r]
+            )
+            for r in range(RB)
+        ]
+
+    def arrive8(k):
         for t in range(2):
             f, s = first[t], second[t]
             o = opp(f)
@@ -278,84 +289,218 @@
             sent(k, t, 17, gs.at[k, t, f])
             sent(k, t, 18, gs.at[k, t, o, lo])
             sent(k, t, 19, gs.at[k, t, o, hi])
-        rhs = weights(k)
+
+    def whole_g(k):
         g0 = jnp.concatenate([gs[k, 0, n // 4, n % 4] for n in range(16)], axis=0)
         g1 = jnp.concatenate([gs[k, 1, n % 4, n // 4] for n in range(16)], axis=0)
-        g = jnp.concatenate([g0, g1], axis=1)
-        term = lax.dot_general(g, rhs, (((1,), (1,)), ((), ())), preferred_element_type=F32)
-        dxa[...] += term.reshape(8, BLK, RB * BLK)
-        wg = jnp.dot(xt[...], g, preferred_element_type=F32)
+        return jnp.concatenate([g0, g1], axis=1)
+
+    def slot_grads(k, g):
+        @pl.when(k >= 2)
+        def _():
+            for d in gw_copies(k - 2):
+                d.wait()
+
+        wg = jnp.dot(xt[...], g, preferred_element_type=F32).astype(BF16)
         for r in range(RB):
             for j in range(2 * WB):
-                gw[r * CBK + 2 * WB * k + j] = wg[r * BLK:(r + 1) * BLK, j * BLK:(j + 1) * BLK]
+                gwst[lax.rem(k, 2), r, j] = wg[r * BLK:(r + 1) * BLK, j * BLK:(j + 1) * BLK]
+        for d in gw_copies(k):
+            d.start()
+
+    def stage8(k):
+        arrive8(k)
+        g = whole_g(k)
+        term = lax.dot_general(
+            g, weights(k), (((1,), (1,)), ((), ())), preferred_element_type=F32
+        )
+        dxa[...] += term.reshape(8, BLK, RB * BLK)
+        slot_grads(k, g)
 
     stages = (stage0, stage1, stage2, stage3, stage4, stage5, stage6, stage7, stage8)
+
+    rhs = weights(0)
+    rows(0, z, rhs)
+    got(2, xh(zl, c, 1))
+    go(9, xh(zl, c, 1), xh(zl, c, 1), sib)
+    got(3, xh(zr, c, 0))
+    go(10, xh(zr, c, 0), xh(zr, c, 0), sib)
+    got(7, xh(zl, 1 - c, 0))
+    got(9, xh(zl, 1 - c, 1))
+    rows(0, zl, rhs)
+    got(8, xh(zr, 1 - c, 1))
+    got(10, xh(zr, 1 - c, 0))
+    rows(0, zr, rhs)
+    got(5, xh(zo, c, 0))
+    go(11, xh(zo, c, 0), xh(zo, c, 0), sib)
+    got(6, xh(zo, c, 1))
+    go(12, xh(zo, c, 1), xh(zo, c, 1), sib)
+    got(11, xh(zo, 1 - c, 0))
+    got(12, xh(zo, 1 - c, 1))
+    rows(0, zo, rhs)
+    send0(0)
+    for d in sends:
+        d.wait_send()
+    sends.clear()
+    gcopy.wait()
+    for r in range(RB):
+        for q in range(8):
+            xt[r * BLK:(r + 1) * BLK, q * BLK:(q + 1) * BLK] = xs[q, :, r * BLK:(r + 1) * BLK].T
 
     def body(i, carry):
         for n in range(len(stages) - 1, -1, -1):
             k = i - n
 
-            @pl.when((k >= 0) & (k < NCH))
+            @pl.when((k >= (0 if n else 1)) & (k < NCH))
             def _():
                 stages[n](k)
 
         return carry
 
-    lax.fori_loop(0, NCH + len(stages) - 1, body, 0)
-
-    sends.clear()
-    for q in range(4):
+    lax.fori_loop(1, NCH + len(stages) - 2, body, 0)
+
+    last = NCH - 1
+    arrive8(last)
+    rhs = weights(last)
+    for n, q in enumerate((zo, zr, zl, z)):
+        g0 = jnp.concatenate([gs[last, 0, q, m] for m in range(4)], axis=0)
+        g1 = jnp.concatenate([gs[last, 1, m, q] for m in range(4)], axis=0)
+        g = jnp.concatenate([g0, g1], axis=1)
+        term = lax.dot_general(g, rhs, (((1,), (1,)), ((), ())), preferred_element_type=F32)
+        dxa[pl.ds(2 * q, 2)] += term.reshape(2, BLK, RB * BLK)
         sb[q] = dxa[2 * q + (1 - c)].astype(BF16)
-    go(9, sb, sr, sib)
-
-    def extract(s, carry):
-        gw_out[s] = gw[cell[s]] * live[s]
-        return carry
-
-    got(9, sr)
-    for q in range(4):
+        go(13 + n, sb.at[q], sr.at[q], sib)
+    lo, hi = pl.ds(0, 64), pl.ds(64, 64)
+
+    def join(n, q):
+        got(13 + n, sr.at[q])
         eb[q] = (dxa[2 * q + c] + sr[q].astype(F32)).astype(BF16)
-    lo, hi = pl.ds(0, 64), pl.ds(64, 64)
-    go(10, eb.at[zo, lo], u1.at[0], zr_dev)
-    go(11, eb.at[zo, hi], u1.at[1], zl_dev)
-    go(12, eb.at[zr, hi], u2.at[0, hi], zr_dev)
-    go(13, eb.at[zl, lo], u2.at[1, lo], zl_dev)
-    lax.fori_loop(0, CAP // 2, extract, 0)
-    got(10, u1.at[0])
+
+    join(0, zo)
+    go(17, eb.at[zo, lo], u1.at[0], zr_dev)
+    go(18, eb.at[zo, hi], u1.at[1], zl_dev)
+    join(1, zr)
+    go(19, eb.at[zr, hi], u2.at[0, hi], zr_dev)
+    join(2, zl)
+    go(20, eb.at[zl, lo], u2.at[1, lo], zl_dev)
+    join(3, z)
+    got(17, u1.at[0])
     eb[zr, lo] = add2(eb[zr, lo], u1[0])
-    go(14, eb.at[zr, lo], u2.at[0, lo], zr_dev)
-    got(11, u1.at[1])
+    go(21, eb.at[zr, lo], u2.at[0, lo], zr_dev)
+    got(18, u1.at[1])
     eb[zl, hi] = add2(eb[zl, hi], u1[1])
-    go(15, eb.at[zl, hi], u2.at[1, hi], zl_dev)
-    lax.fori_loop(CAP // 2, CAP, extract, 0)
-    got(12, u2.at[0, hi])
-    got(13, u2.at[1, lo])
-    got(14, u2.at[0, lo])
-    got(15, u2.at[1, hi])
+    go(22, eb.at[zl, hi], u2.at[1, hi], zl_dev)
+    slot_grads(last, whole_g(last))
+    for k in range(NCH - SL, NCH):
+        for t in range(2):
+            cols = pl.ds((2 * k + t) * W, W)
+            pltpu.make_async_copy(
+                act.at[k % SL, t], act_hbm.at[:, cols], osem.at[k % SL, t]
+            ).wait()
+    for k in (last - 1, last):
+        for d in gw_copies(k):
+            d.wait()
+    got(19, u2.at[0, hi])
+    got(20, u2.at[1, lo])
+    got(21, u2.at[0, lo])
+    got(22, u2.at[1, hi])
     dx_out[...] = eb[z].astype(F32) + u2[0].astype(F32) + u2[1].astype(F32)
     for d in sends:
         d.wait_send()
 
 
+def table_kernel(rows, cols, count, idx):
+    row0 = lax.axis_index("inb") * RB
+    col0 = lax.axis_index("outb") * CBK
+
+    def clear(n, carry):
+        idx[n] = CAP
+        return carry
+
+    lax.fori_loop(0, RB * CBK, clear, 0, unroll=8)
+
+    def put(s, carry):
+        idx[(rows[s] - row0) * CBK + cols[s] - col0] = s
+        return carry
+
+    lax.fori_loop(0, count[0, 0], put, 0)
+
+
+def pick_kernel(rows, cols, count, act_in, dx_in, gwd, act, dx, gw, abuf, dbuf, gbuf, obuf, sem, gsem, osem):
+    row0 = lax.axis_index("inb") * RB
+    col0 = lax.axis_index("outb") * CBK
+
+    def fetch(s):
+        cell = (rows[s] - row0) * CBK + cols[s] - col0
+        return pltpu.make_async_copy(gwd.at[cell], gbuf.at[s], gsem.at[s])
+
+    def begin(s, carry):
+        fetch(s).start()
+        return carry
+
+    lax.fori_loop(0, CAP, begin, 0, unroll=4)
+    ins = [
+        pltpu.make_async_copy(act_in, abuf, sem.at[0]),
+        pltpu.make_async_copy(dx_in, dbuf, sem.at[1]),
+    ]
+    for d in ins:
+        d.start()
+    outs = [
+        pltpu.make_async_copy(abuf, act, sem.at[2]),
+        pltpu.make_async_copy(dbuf, dx, sem.at[3]),
+    ]
+
+    def flush(n):
+        return pltpu.make_async_copy(
+            obuf.at[pl.ds(n * 8, 8)], gw.at[pl.ds(n * 8, 8)], osem.at[n]
+        )
+
+    def group(n, carry):
+        for m in range(8):
+            s = n * 8 + m
+            fetch(s).wait()
+            alive = (s < count[0, 0]).astype(F32)
+            obuf[s] = gbuf[s].astype(F32) * alive
+        flush(n).start()
+        return carry
+
+    lax.fori_loop(0, CAP // 8, group, 0)
+    for d, e in zip(ins, outs):
+        d.wait()
+        e.start()
+
+    def done(n, carry):
+        flush(n).wait()
+        return carry
+
+    lax.fori_loop(0, CAP // 8, done, 0)
+    for e in outs:
+        e.wait()
+
+
 def per_device(tokens, weight_blocks, block_rows, block_cols, block_count, grad_act):
-    slot_ids = jnp.arange(CAP, dtype=jnp.int32)
-    row_local = block_rows[0, 0] - lax.axis_index("inb") * RB
-    col_local = block_cols[0, 0] - lax.axis_index("outb") * CBK
-    is_live = slot_ids < block_count[0, 0]
-    cell = row_local * CBK + col_local
-    hit = (jnp.arange(RB * CBK, dtype=jnp.int32)[:, None] == cell[None, :]) & is_live[None, :]
-    idx = CAP - jnp.sum(jnp.where(hit, CAP - slot_ids[None, :], 0), axis=1)
     vmem = pl.BlockSpec(memory_space=pltpu.VMEM)
     smem = pl.BlockSpec(memory_space=pltpu.SMEM)
-    out = pl.pallas_call(
+    hbm = pl.BlockSpec(memory_space=pl.ANY)
+    rows, cols, count = block_rows[0, 0], block_cols[0, 0], block_count
+    act_shape = jax.ShapeDtypeStruct((64, CBK * BLK), BF16)
+    dx_shape = jax.ShapeDtypeStruct((BLK, RB * BLK), F32)
+    idx = pl.pallas_call(
+        table_kernel,
+        out_shape=jax.ShapeDtypeStruct((RB * CBK,), jnp.int32),
+        in_specs=[smem, smem, smem],
+        out_specs=smem,
+        name="table",
+    )(rows, cols, count)
+    act, dx, gwd = pl.pallas_call(
         kernel,
         out_shape=(
-            jax.ShapeDtypeStruct((64, CBK * BLK), BF16),
-            jax.ShapeDtypeStruct((BLK, RB * BLK), F32),
-            jax.ShapeDtypeStruct((CAP, BLK, BLK), F32),
+            act_shape,
+            dx_shape,
+            jax.ShapeDtypeStruct((RB * CBK, BLK, BLK), BF16),
         ),
-        in_specs=[smem, smem, smem, vmem, pl.BlockSpec(memory_space=pl.ANY), vmem],
-        out_specs=(vmem, vmem, vmem),
+        in_specs=[smem, hbm, hbm, hbm],
+        out_specs=(hbm, vmem, hbm),
         scratch_shapes=[
             pltpu.VMEM((CAP + 1, BLK, BLK), BF16),
             pltpu.VMEM((8, BLK, RB * BLK), BF16),
@@ -368,7 +513,9 @@
             pltpu.VMEM((SL, 2, 2, 64, W), BF16),
             pltpu.VMEM((NCH, 2, 4, 4, 64, W), BF16),
             pltpu.VMEM((8, BLK, RB * BLK), F32),
-            pltpu.VMEM((RB * CBK, BLK, BLK), F32),
+            pltpu.VMEM((64, CBK * BLK), BF16),
+            pltpu.VMEM((SL, 2, 64, W), BF16),
+            pltpu.VMEM((2, RB, 2 * WB, BLK, BLK), BF16),
             pltpu.VMEM((4, BLK, RB * BLK), BF16),
             pltpu.VMEM((4, BLK, RB * BLK), BF16),
             pltpu.VMEM((4, BLK, RB * BLK), BF16),
@@ -376,17 +523,35 @@
             pltpu.VMEM((2, BLK, RB * BLK), BF16),
             pltpu.SemaphoreType.DMA((SL, 2, 20)),
             pltpu.SemaphoreType.DMA((SL, 2, 20)),
-            pltpu.SemaphoreType.DMA((16,)),
-            pltpu.SemaphoreType.DMA((16,)),
-            pltpu.SemaphoreType.DMA((2,)),
+            pltpu.SemaphoreType.DMA((23,)),
+            pltpu.SemaphoreType.DMA((23,)),
+            pltpu.SemaphoreType.DMA((3,)),
+            pltpu.SemaphoreType.DMA((SL, 2)),
+            pltpu.SemaphoreType.DMA((2, RB)),
         ],
         compiler_params=pltpu.CompilerParams(
             collective_id=0, has_side_effects=True, vmem_limit_bytes=67043328
         ),
         name="ffn",
-    )(idx, cell, is_live.astype(F32), tokens, weight_blocks[0, 0], grad_act)
-    activation, grad_tokens, grad_weights = out
-    return (activation, grad_tokens, grad_weights[None, None])
+    )(idx, tokens, weight_blocks[0, 0], grad_act)
+    act, dx, gw = pl.pallas_call(
+        pick_kernel,
+        out_shape=(act_shape, dx_shape, jax.ShapeDtypeStruct((CAP, BLK, BLK), F32)),
+        in_specs=[smem, smem, smem, hbm, hbm, hbm],
+        out_specs=(hbm, hbm, hbm),
+        scratch_shapes=[
+            pltpu.VMEM(act_shape.shape, BF16),
+            pltpu.VMEM(dx_shape.shape, F32),
+            pltpu.VMEM((CAP, BLK, BLK), BF16),
+            pltpu.VMEM((CAP, BLK, BLK), F32),
+            pltpu.SemaphoreType.DMA((4,)),
+            pltpu.SemaphoreType.DMA((CAP,)),
+            pltpu.SemaphoreType.DMA((CAP // 8,)),
+        ],
+        compiler_params=pltpu.CompilerParams(vmem_limit_bytes=67043328),
+        name="pick",
+    )(rows, cols, count, act, dx, gwd)
+    return (act, dx, gw[None, None])
 
 
 def solution(mesh):

time: 188 us -> 179 us (0.952)
  local copies, waits for them, and re-layouts: 8.92 us -> 0 us
  Pallas kernels: 174 us -> 177 us
  other arithmetic: 1.89 us -> 0 us
    unnamed x5 -> x0, local copies, waits for them, and re-layouts: 8.92 us -> none
    pallas_call x1 -> x3, Pallas kernels: 174 us -> 177 us  [the longest x1 170 us: per_device(): pl.pallas_call(kernel, out_shape=(act_shape, dx_shape, jax.ShapeDtypeStru...]
where the time goes in v2:
time: 179 us
  Pallas kernels  177 us (99%)
    pallas_call x1, Pallas kernels, per_device(): pl.pallas_call(kernel, out_shape=(act_shape, dx_shape, jax.ShapeDtypeStru...  170 us
    pallas_call x1, Pallas kernels, per_device(): pl.pallas_call(pick_kernel, out_shape=(act_shape, dx_shape, jax.ShapeDtyp...  4.9 us

profile of v2, /device:TPU:0, one launch (start us, length us, event | category | flops | bytes accessed | tf_op | source)
XLA Modules:
  0.0 178.6 jit_solution(13295146713034556240)
XLA Ops:
  1.3 2.2 %table.1.idx = s32[288]{0:T(512)} custom-call(s32[72]{0:T(128)} %bitcast.5, s32[72]{0:T(128)} %bitcast.7, s32[1,1]{1,0:T(1,128)S(6)} %copy.9.count), custom_call_target="tpu_custom_call" | custom-call | tf_op jit(solution)/shard_map/table/pallas_call | solution.py:488
  3.5 170.2 %ffn.1 = (bf16[64,6144]{1,0:T(8,128)(2,1)}, f32[128,768]{1,0:T(8,128)}, bf16[288,128,128]{2,1,0:T(8,128)(2,1)}) custom-call(s32[288]{0:T(512)} %table.1.idx, bf16[128,768]{1,0:T(8,128)(2,1)} %tok.1, bf16[72,128,128]{2,1,0:T(8,128)(2,1)} %bitcast.4, bf16[64,6144]{1,0:T(8,128)(2,1)} %gact_hbm.1), custom_call_target="tpu_custom_call" | custom-call | tf_op jit(solution)/shard_map/ffn/pallas_call | solution.py:495
  173.7 4.9 %pick.1 = (bf16[64,6144]{1,0:T(8,128)(2,1)}, f32[128,768]{1,0:T(8,128)}, f32[72,128,128]{2,1,0:T(8,128)}) custom-call(s32[72]{0:T(128)} %bitcast.6, s32[72]{0:T(128)} %bitcast.8, s32[1,1]{1,0:T(1,128)S(6)} %copy.9.count, bf16[64,6144]{1,0:T(8,128)(2,1)} %get-tuple-element.9.act_in, f32[128,768]{1,0:T(8,128)} %get-tuple-element.10.dx_in, ...), custom_call_target="tpu_custom_call" | custom-call | tf_op jit(solution)/shard_map/pick/pallas_call | solution.py:537

commit v3 on v2

--- a/solution.py
+++ b/solution.py
@@ -16,7 +16,7 @@
 RB = 6
 CBK = 48
 CAP = 72
-WB = 2
+WB = 3
 W = WB * BLK
 NCH = CBK // (2 * WB)
 SL = 4
@@ -27,8 +27,9 @@
 
 
 def kernel(
-    idx, tok, wblk, gact_hbm,
+    rows_in, cols_in, count_in, tok, wblk, gact_hbm,
     act_hbm, dx_out, gw_hbm,
+    idx, tbl,
     wp, xs, xt, ps, r1, r2, qs, t1, t2, gs, dxa, gact, act, gwst, sb, sr, eb, u1, u2,
     ssem, rsem, asem, arsem, lsem, osem, gsem,
 ):
@@ -74,6 +75,17 @@
     ):
         pl.semaphore_signal(barrier, inc=1, device_id=dev, device_id_type=MESH)
     wp[CAP] = jnp.zeros((BLK, BLK), BF16)
+
+    flat = BLK * lax.broadcasted_iota(jnp.int32, (8, BLK), 0) + lax.broadcasted_iota(jnp.int32, (8, BLK), 1)
+
+    def place(n, found):
+        cell = (rows_in[n] - a * RB) * CBK + cols_in[n] - b * CBK
+        cell = jnp.where(n < count_in[0, 0], cell, 8 * BLK)
+        return jnp.where(flat == cell, n, found)
+
+    tbl[...] = lax.fori_loop(0, CAP, place, jnp.full((8, BLK), CAP, jnp.int32), unroll=4)
+    tcopy = pltpu.make_async_copy(tbl, idx, lsem.at[3])
+    tcopy.start()
     pl.semaphore_wait(barrier, 7)
 
     def ac(n, src, dst, dev):
@@ -85,8 +97,8 @@
     def xb(zz, cc):
         return xs.at[2 * zz + cc]
 
-    def xh(zz, cc, h):
-        return xs.at[2 * zz + cc, pl.ds(64 * h, 64)]
+    def xq(zz, cc, h):
+        return xs.at[2 * zz + cc, pl.ds(32 * h, 32)]
 
     sends = []
 
@@ -98,28 +110,29 @@
     def got(n, dst):
         ac(n, dst, dst, sib).wait_recv()
 
-    th = [tok.at[pl.ds(0, 64)], tok.at[pl.ds(64, 64)]]
-    go(0, th[0], xh(z, c, 0), zr_dev)
-    go(1, th[1], xh(z, c, 1), zl_dev)
-    go(2, th[1], xh(z, c, 1), zr_dev)
-    go(3, th[0], xh(z, c, 0), zl_dev)
-    go(4, tok, xb(z, c), sib)
+    for n in range(4):
+        m = (n + 2) % 4
+        go(n, tok.at[pl.ds(32 * n, 32)], xq(z, c, n), zr_dev)
+        go(4 + n, tok.at[pl.ds(32 * m, 32)], xq(z, c, m), zl_dev)
+    go(8, tok, xb(z, c), sib)
     dxa[...] = jnp.zeros_like(dxa)
-    got(0, xh(zl, c, 0))
-    go(5, xh(zl, c, 0), xh(zl, c, 0), zr_dev)
-    got(1, xh(zr, c, 1))
-    go(6, xh(zr, c, 1), xh(zr, c, 1), zl_dev)
-    go(7, xh(zl, c, 0), xh(zl, c, 0), sib)
-    go(8, xh(zr, c, 1), xh(zr, c, 1), sib)
+    for n in range(2):
+        got(n, xq(zl, c, n))
+        go(9 + n, xq(zl, c, n), xq(zl, c, n), zr_dev)
+        got(4 + n, xq(zr, c, n + 2))
+        go(11 + n, xq(zr, c, n + 2), xq(zr, c, n + 2), zl_dev)
+        go(13 + n, xq(zl, c, n), xq(zl, c, n), sib)
+        go(15 + n, xq(zr, c, n + 2), xq(zr, c, n + 2), sib)
     xcopy.wait()
     wcopy.wait()
-    got(4, xb(z, 1 - c))
+    tcopy.wait()
+    got(8, xb(z, 1 - c))
 
     def weights(k):
         cols = []
         for j in range(2 * WB):
             col = 2 * WB * k + j
-            cols.append(jnp.concatenate([wp[idx[r * CBK + col]] for r in range(RB)], axis=0))
+            cols.append(jnp.concatenate([wp[idx[(r * CBK + col) // BLK, (r * CBK + col) % BLK]] for r in range(RB)], axis=0))
         return jnp.concatenate(cols, axis=1)
 
     def copy(k, t, n, src, dst, dev):
@@ -321,33 +334,41 @@
 
     rhs = weights(0)
     rows(0, z, rhs)
-    got(2, xh(zl, c, 1))
-    go(9, xh(zl, c, 1), xh(zl, c, 1), sib)
-    got(3, xh(zr, c, 0))
-    go(10, xh(zr, c, 0), xh(zr, c, 0), sib)
-    got(7, xh(zl, 1 - c, 0))
-    got(9, xh(zl, 1 - c, 1))
+    for n in range(2):
+        got(2 + n, xq(zl, c, n + 2))
+        go(17 + n, xq(zl, c, n + 2), xq(zl, c, n + 2), sib)
+        got(6 + n, xq(zr, c, n))
+        go(19 + n, xq(zr, c, n), xq(zr, c, n), sib)
+    for n in range(2):
+        got(9 + n, xq(zo, c, n))
+        go(21 + n, xq(zo, c, n), xq(zo, c, n), sib)
+        got(11 + n, xq(zo, c, n + 2))
+        go(23 + n, xq(zo, c, n + 2), xq(zo, c, n + 2), sib)
+    for n in range(2):
+        got(13 + n, xq(zl, 1 - c, n))
+        got(17 + n, xq(zl, 1 - c, n + 2))
     rows(0, zl, rhs)
-    got(8, xh(zr, 1 - c, 1))
-    got(10, xh(zr, 1 - c, 0))
+    for n in range(2):
+        got(15 + n, xq(zr, 1 - c, n + 2))
+        got(19 + n, xq(zr, 1 - c, n))
     rows(0, zr, rhs)
-    got(5, xh(zo, c, 0))
-    go(11, xh(zo, c, 0), xh(zo, c, 0), sib)
-    got(6, xh(zo, c, 1))
-    go(12, xh(zo, c, 1), xh(zo, c, 1), sib)
-    got(11, xh(zo, 1 - c, 0))
-    got(12, xh(zo, 1 - c, 1))
+    for n in range(2):
+        got(21 + n, xq(zo, 1 - c, n))
+        got(23 + n, xq(zo, 1 - c, n + 2))
     rows(0, zo, rhs)
     send0(0)
     for d in sends:
         d.wait_send()
     sends.clear()
     gcopy.wait()
-    for r in range(RB):
-        for q in range(8):
-            xt[r * BLK:(r + 1) * BLK, q * BLK:(q + 1) * BLK] = xs[q, :, r * BLK:(r + 1) * BLK].T
 
     def body(i, carry):
+        @pl.when(i == 2)
+        def _():
+            for r in range(RB):
+                for q in range(8):
+                    xt[r * BLK:(r + 1) * BLK, q * BLK:(q + 1) * BLK] = xs[q, :, r * BLK:(r + 1) * BLK].T
+
         for n in range(len(stages) - 1, -1, -1):
             k = i - n
 
@@ -369,27 +390,27 @@
         term = lax.dot_general(g, rhs, (((1,), (1,)), ((), ())), preferred_element_type=F32)
         dxa[pl.ds(2 * q, 2)] += term.reshape(2, BLK, RB * BLK)
         sb[q] = dxa[2 * q + (1 - c)].astype(BF16)
-        go(13 + n, sb.at[q], sr.at[q], sib)
+        go(25 + n, sb.at[q], sr.at[q], sib)
     lo, hi = pl.ds(0, 64), pl.ds(64, 64)
 
     def join(n, q):
-        got(13 + n, sr.at[q])
+        got(25 + n, sr.at[q])
         eb[q] = (dxa[2 * q + c] + sr[q].astype(F32)).astype(BF16)
 
     join(0, zo)
-    go(17, eb.at[zo, lo], u1.at[0], zr_dev)
-    go(18, eb.at[zo, hi], u1.at[1], zl_dev)
+    go(29, eb.at[zo, lo], u1.at[0], zr_dev)
+    go(30, eb.at[zo, hi], u1.at[1], zl_dev)
     join(1, zr)
-    go(19, eb.at[zr, hi], u2.at[0, hi], zr_dev)
+    go(31, eb.at[zr, hi], u2.at[0, hi], zr_dev)
     join(2, zl)
-    go(20, eb.at[zl, lo], u2.at[1, lo], zl_dev)
+    go(32, eb.at[zl, lo], u2.at[1, lo], zl_dev)
     join(3, z)
-    got(17, u1.at[0])
+    got(29, u1.at[0])
     eb[zr, lo] = add2(eb[zr, lo], u1[0])
-    go(21, eb.at[zr, lo], u2.at[0, lo], zr_dev)
-    got(18, u1.at[1])
+    go(33, eb.at[zr, lo], u2.at[0, lo], zr_dev)
+    got(30, u1.at[1])
     eb[zl, hi] = add2(eb[zl, hi], u1[1])
-    go(22, eb.at[zl, hi], u2.at[1, hi], zl_dev)
+    go(34, eb.at[zl, hi], u2.at[1, hi], zl_dev)
     slot_grads(last, whole_g(last))
     for k in range(NCH - SL, NCH):
         for t in range(2):
@@ -400,30 +421,13 @@
     for k in (last - 1, last):
         for d in gw_copies(k):
             d.wait()
-    got(19, u2.at[0, hi])
-    got(20, u2.at[1, lo])
-    got(21, u2.at[0, lo])
-    got(22, u2.at[1, hi])
+    got(31, u2.at[0, hi])
+    got(32, u2.at[1, lo])
+    got(33, u2.at[0, lo])
+    got(34, u2.at[1, hi])
     dx_out[...] = eb[z].astype(F32) + u2[0].astype(F32) + u2[1].astype(F32)
     for d in sends:
         d.wait_send()
-
-
-def table_kernel(rows, cols, count, idx):
-    row0 = lax.axis_index("inb") * RB
-    col0 = lax.axis_index("outb") * CBK
-
-    def clear(n, carry):
-        idx[n] = CAP
-        return carry
-
-    lax.fori_loop(0, RB * CBK, clear, 0, unroll=8)
-
-    def put(s, carry):
-        idx[(rows[s] - row0) * CBK + cols[s] - col0] = s
-        return carry
-
-    lax.fori_loop(0, count[0, 0], put, 0)
 
 
 def pick_kernel(rows, cols, count, act_in, dx_in, gwd, act, dx, gw, abuf, dbuf, gbuf, obuf, sem, gsem, osem):
@@ -485,13 +489,6 @@
     rows, cols, count = block_rows[0, 0], block_cols[0, 0], block_count
     act_shape = jax.ShapeDtypeStruct((64, CBK * BLK), BF16)
     dx_shape = jax.ShapeDtypeStruct((BLK, RB * BLK), F32)
-    idx = pl.pallas_call(
-        table_kernel,
-        out_shape=jax.ShapeDtypeStruct((RB * CBK,), jnp.int32),
-        in_specs=[smem, smem, smem],
-        out_specs=smem,
-        name="table",
-    )(rows, cols, count)
     act, dx, gwd = pl.pallas_call(
         kernel,
         out_shape=(
@@ -499,9 +496,11 @@
             dx_shape,
             jax.ShapeDtypeStruct((RB * CBK, BLK, BLK), BF16),
         ),
-        in_specs=[smem, hbm, hbm, hbm],
+        in_specs=[smem, smem, smem, hbm, hbm, hbm],
         out_specs=(hbm, vmem, hbm),
         scratch_shapes=[
+            pltpu.SMEM((8, BLK), jnp.int32),
+            pltpu.VMEM((8, BLK), jnp.int32),
             pltpu.VMEM((CAP + 1, BLK, BLK), BF16),
             pltpu.VMEM((8, BLK, RB * BLK), BF16),
             pltpu.VMEM((RB * BLK, 1024), BF16),
@@ -523,9 +522,9 @@
             pltpu.VMEM((2, BLK, RB * BLK), BF16),
             pltpu.SemaphoreType.DMA((SL, 2, 20)),
             pltpu.SemaphoreType.DMA((SL, 2, 20)),
-            pltpu.SemaphoreType.DMA((23,)),
-            pltpu.SemaphoreType.DMA((23,)),
-            pltpu.SemaphoreType.DMA((3,)),
+            pltpu.SemaphoreType.DMA((35,)),
+            pltpu.SemaphoreType.DMA((35,)),
+            pltpu.SemaphoreType.DMA((4,)),
             pltpu.SemaphoreType.DMA((SL, 2)),
             pltpu.SemaphoreType.DMA((2, RB)),
         ],
@@ -533,7 +532,7 @@
             collective_id=0, has_side_effects=True, vmem_limit_bytes=67043328
         ),
         name="ffn",
-    )(idx, tokens, weight_blocks[0, 0], grad_act)
+    )(rows, cols, count, tokens, weight_blocks[0, 0], grad_act)
     act, dx, gw = pl.pallas_call(
         pick_kernel,
         out_shape=(act_shape, dx_shape, jax.ShapeDtypeStruct((CAP, BLK, BLK), F32)),

time: 179 us -> 174 us (0.972)
  Pallas kernels: 177 us -> 173 us
    pallas_call x1 -> x0, Pallas kernels: 2.21 us -> none  [per_device(): pl.pallas_call(table_kernel, out_shape=jax.ShapeDtypeStruct((RB * CBK,),...]
    pallas_call x1, Pallas kernels: 170 us -> 168 us  [per_device(): pl.pallas_call(kernel, out_shape=(act_shape, dx_shape, jax.ShapeDtypeStru...]
where the time goes in v3:
time: 174 us
  Pallas kernels  173 us (99%)
    pallas_call x1, Pallas kernels, per_device(): pl.pallas_call(kernel, out_shape=(act_shape, dx_shape, jax.ShapeDtypeStru...  168 us
    pallas_call x1, Pallas kernels, per_device(): pl.pallas_call(pick_kernel, out_shape=(act_shape, dx_shape, jax.ShapeDtyp...  4.9 us

profile of v3, /device:TPU:0, one launch (start us, length us, event | category | flops | bytes accessed | tf_op | source)
XLA Modules:
  0.0 174.1 jit_solution(17434349405389149520)
XLA Ops:
  1.3 168.0 %ffn.1 = (bf16[64,6144]{1,0:T(8,128)(2,1)}, f32[128,768]{1,0:T(8,128)}, bf16[288,128,128]{2,1,0:T(8,128)(2,1)}) custom-call(s32[72]{0:T(128)} %bitcast.5, s32[72]{0:T(128)} %bitcast.7, s32[1,1]{1,0:T(1,128)S(6)} %copy.9.count_in.count, bf16[128,768]{1,0:T(8,128)(2,1)} %tok.1, bf16[72,128,128]{2,1,0:T(8,128)(2,1)} %bitcast.4, bf16[64,6144]{1,0:T(8,128)(2,1)} %gact_hbm.1), custom_call_target="tpu_custom_call" | custom-call | tf_op jit(solution)/shard_map/ffn/pallas_call | solution.py:492
  169.2 4.9 %pick.1 = (bf16[64,6144]{1,0:T(8,128)(2,1)}, f32[128,768]{1,0:T(8,128)}, f32[72,128,128]{2,1,0:T(8,128)}) custom-call(s32[72]{0:T(128)} %bitcast.6, s32[72]{0:T(128)} %bitcast.8, s32[1,1]{1,0:T(1,128)S(6)} %copy.9.count_in.count, bf16[64,6144]{1,0:T(8,128)(2,1)} %get-tuple-element.9.act_in, f32[128,768]{1,0:T(8,128)} %get-tuple-element.10.dx_in, ...), custom_call_target="tpu_custom_call" | custom-call | tf_op jit(solution)/shard_map/pick/pallas_call | solution.py:536

commit v4 on v3

v4 whole, which is shorter than its diff:
```python
import functools

import jax
import jax.numpy as jnp
from jax import lax
from jax.experimental import pallas as pl
from jax.experimental.pallas import tpu as pltpu
from jax.sharding import PartitionSpec as P

MESH = pl.DeviceIdType.MESH
F32 = jnp.float32
BF16 = jnp.bfloat16
INV_ROOT_TWO = 0.7071067811865476
INV_ROOT_TAU = 0.3989422804014327
BLK = 128
RB = 6
CBK = 48
CAP = 72
WB = 3
W = WB * BLK
NCH = CBK // (2 * WB)
SL = 4
EARLY = 1


def add2(a, b):
    return (a.astype(F32) + b.astype(F32)).astype(BF16)


def kernel(
    rows_in, cols_in, count_in, tok, wblk, gact_hbm,
    act_hbm, dx_out, gw_hbm,
    idx, tbl,
    wp, xs, xt, ps, r1, r2, qs, t1, t2, gs, dxa, gact, act, gwst, sb, sr, eb, u1, u2,
    ssem, rsem, asem, arsem, lsem, osem, gsem,
):
    a = lax.axis_index("inb")
    b = lax.axis_index("outb")
    x, y = a // 4, a % 4
    z, c = b // 2, b % 2

    def up(v):
        return lax.rem(v + 1, 4)

    def down(v):
        return lax.rem(v + 3, 4)

    def opp(v):
        return lax.rem(v + 2, 4)

    zr, zl = up(z), down(z)
    sib = (a, 2 * z + (1 - c))
    zr_dev, zl_dev = (a, 2 * zr + c), (a, 2 * zl + c)

    xr = lax.rem(x - z + 5, 4)
    first = (xr, y)
    second = (y, xr)

    def dev_x(v):
        return (4 * lax.rem(v + z + 3, 4) + y, b)

    def dev_y(v):
        return (4 * x + v, b)

    def dev_first(t, v):
        return dev_x(v) if t == 0 else dev_y(v)

    def dev_second(t, v):
        return dev_y(v) if t == 0 else dev_x(v)

    wcopy = pltpu.make_async_copy(wblk, wp.at[pl.ds(0, CAP)], lsem.at[0])
    wcopy.start()
    xcopy = pltpu.make_async_copy(tok, xs.at[2 + c], lsem.at[1])
    xcopy.start()
    gcopy = pltpu.make_async_copy(gact_hbm, gact, lsem.at[2])
    gcopy.start()

    barrier = pltpu.get_barrier_semaphore()
    for dev in (
        dev_x(up(xr)), dev_x(down(xr)), dev_y(up(y)), dev_y(down(y)),
        zr_dev, zl_dev, sib,
    ):
        pl.semaphore_signal(barrier, inc=1, device_id=dev, device_id_type=MESH)
    wp[CAP] = jnp.zeros((BLK, BLK), BF16)

    flat = BLK * lax.broadcasted_iota(jnp.int32, (8, BLK), 0) + lax.broadcasted_iota(jnp.int32, (8, BLK), 1)

    def place(n, found):
        cell = (rows_in[n] - a * RB) * CBK + cols_in[n] - b * CBK
        cell = jnp.where(n < count_in[0, 0], cell, 8 * BLK)
        return jnp.where(flat == cell, n, found)

    tbl[...] = lax.fori_loop(0, CAP, place, jnp.full((8, BLK), CAP, jnp.int32), unroll=4)
    tcopy = pltpu.make_async_copy(tbl, idx, lsem.at[3])
    tcopy.start()
    pl.semaphore_wait(barrier, 7)

    def ac(part, n, src, dst, dev):
        return pltpu.make_async_remote_copy(
            src_ref=src, dst_ref=dst, send_sem=asem.at[part], recv_sem=arsem.at[n],
            device_id=dev, device_id_type=MESH,
        )

    def go(part, n, src, dst, dev):
        ac(part, n, src, dst, dev).start()

    def got(n, dst):
        ac(0, n, dst, dst, sib).wait_recv()

    def xq(j, cc, h):
        return xs.at[2 * j + cc, pl.ds(32 * h, 32)]

    for n in range(4):
        m = (n + 2) % 4
        go(0, n, tok.at[pl.ds(32 * n, 32)], xq(0, c, n), zr_dev)
        go(0, 4 + m, tok.at[pl.ds(32 * m, 32)], xq(2, c, m), zl_dev)
    go(0, 8, tok, xs.at[2 + c], sib)
    dxa[...] = jnp.zeros_like(dxa)
    xcopy.wait()
    wcopy.wait()
    tcopy.wait()
    got(8, xs.at[2 + 1 - c])

    def weights(k):
        cols = []
        for j in range(2 * WB):
            col = 2 * WB * k + j
            cols.append(jnp.concatenate([wp[idx[(r * CBK + col) // BLK, (r * CBK + col) % BLK]] for r in range(RB)], axis=0))
        return jnp.concatenate(cols, axis=1)

    def copy(k, t, part, n, src, dst, dev):
        slot = lax.rem(k, SL)
        return pltpu.make_async_remote_copy(
            src_ref=src, dst_ref=dst,
            send_sem=ssem.at[slot, t, part], recv_sem=rsem.at[slot, t, n],
            device_id=dev, device_id_type=MESH,
        )

    def start(k, t, n, src, dst, dev):
        copy(k, t, n // 3, n, src, dst, dev).start()

    def arrived(k, t, n, dst):
        copy(k, t, n // 3, n, dst, dst, sib).wait_recv()

    def sent(k, t, part, src):
        copy(k, t, part, 3 * part, src, src, sib).wait_send()

    def rows(slot, m, rhs):
        lhs = jnp.concatenate([xs[2 * m], xs[2 * m + 1]], axis=0)
        out = jnp.dot(lhs, rhs, preferred_element_type=F32).astype(BF16)
        for n in range(4):
            ps[slot, 0, m, n] = out[64 * n:64 * n + 64, :W]
            ps[slot, 1, n, m] = out[64 * n:64 * n + 64, W:]

    def stage0(k):
        rhs = weights(k)
        for m in range(4):
            rows(lax.rem(k, SL), m, rhs)
        send0(k)

    def push(k, t, n):
        slot = lax.rem(k, SL)
        f = first[t]
        r, l, o = up(f), down(f), opp(f)
        lo, hi = pl.ds(0, 2), pl.ds(2, 2)
        if n == 0:
            start(k, t, 0, ps.at[slot, t, o, lo], r1.at[slot, t, 0], dev_first(t, r))
        elif n == 1:
            start(k, t, 1, ps.at[slot, t, o, hi], r1.at[slot, t, 1], dev_first(t, l))
        elif n == 2:
            start(k, t, 2, ps.at[slot, t, r, hi], r2.at[slot, t, 0, hi], dev_first(t, r))
        else:
            start(k, t, 2, ps.at[slot, t, l, lo], r2.at[slot, t, 1, lo], dev_first(t, l))

    def send0(k):
        for t in range(2):
            for n in range(4):
                push(k, t, n)

    def stage1(k):
        slot = lax.rem(k, SL)
        for t in range(2):
            f = first[t]
            r, l = up(f), down(f)
            lo, hi = pl.ds(0, 2), pl.ds(2, 2)
            arrived(k, t, 0, r1.at[slot, t, 0])
            ps[slot, t, r, lo] = add2(ps[slot, t, r, lo], r1[slot, t, 0])
            start(k, t, 2, ps.at[slot, t, r, lo], r2.at[slot, t, 0, lo], dev_first(t, r))
            arrived(k, t, 1, r1.at[slot, t, 1])
            ps[slot, t, l, hi] = add2(ps[slot, t, l, hi], r1[slot, t, 1])
            start(k, t, 2, ps.at[slot, t, l, hi], r2.at[slot, t, 1, hi], dev_first(t, l))

    def stage2(k):
        slot = lax.rem(k, SL)
        for t in range(2):
            f, s = first[t], second[t]
            arrived(k, t, 2, r2.at[slot, t])
            qs[slot, t] = (
                ps[slot, t, f].astype(F32) + r2[slot, t, 0].astype(F32) + r2[slot, t, 1].astype(F32)
            ).astype(BF16)
            sent(k, t, 0, ps.at[slot, t, pl.ds(0, 3)])
            r, l, o = up(s), down(s), opp(s)
            lo, hi = pl.ds(0, 32), pl.ds(32, 32)
            start(k, t, 3, qs.at[slot, t, o, lo], t1.at[slot, t, 0], dev_second(t, r))
            start(k, t, 4, qs.at[slot, t, o, hi], t1.at[slot, t, 1], dev_second(t, l))
            start(k, t, 5, qs.at[slot, t, r, hi], t2.at[slot, t, 0, hi], dev_second(t, r))
            start(k, t, 5, qs.at[slot, t, l, lo], t2.at[slot, t, 1, lo], dev_second(t, l))

    def stage3(k):
        slot = lax.rem(k, SL)
        for t in range(2):
            s = second[t]
            r, l = up(s), down(s)
            lo, hi = pl.ds(0, 32), pl.ds(32, 32)
            arrived(k, t, 3, t1.at[slot, t, 0])
            qs[slot, t, r, lo] = add2(qs[slot, t, r, lo], t1[slot, t, 0])
            start(k, t, 5, qs.at[slot, t, r, lo], t2.at[slot, t, 0, lo], dev_second(t, r))
            arrived(k, t, 4, t1.at[slot, t, 1])
            qs[slot, t, l, hi] = add2(qs[slot, t, l, hi], t1[slot, t, 1])
            start(k, t, 5, qs.at[slot, t, l, hi], t2.at[slot, t, 1, hi], dev_second(t, l))

    def stage4(k):
        slot = lax.rem(k, SL)
        for t in range(2):
            f, s = first[t], second[t]
            arrived(k, t, 5, t2.at[slot, t])
            pre = qs[slot, t, s].astype(F32) + t2[slot, t, 0].astype(F32) + t2[slot, t, 1].astype(F32)
            cdf = 0.5 * (1.0 + lax.erf(pre * INV_ROOT_TWO))
            cols = pl.ds(pl.multiple_of((2 * k + t) * W, W), W)
            slope = cdf + pre * jnp.exp(-0.5 * pre * pre) * INV_ROOT_TAU
            gs[k, t, f, s] = (gact[:, cols].astype(F32) * slope).astype(BF16)
            sent(k, t, 1, qs.at[slot, t, pl.ds(0, 3)])
            start(k, t, 6, gs.at[k, t, f, s], gs.at[k, t, f, s], dev_second(t, up(s)))
            start(k, t, 7, gs.at[k, t, f, s], gs.at[k, t, f, s], dev_second(t, down(s)))

            @pl.when(k >= SL)
            def _():
                pltpu.make_async_copy(act.at[slot, t], act_hbm.at[:, cols], osem.at[slot, t]).wait()

            act[slot, t] = (pre * cdf).astype(BF16)
            pltpu.make_async_copy(act.at[slot, t], act_hbm.at[:, cols], osem.at[slot, t]).start()

    def stage5(k):
        for t in range(2):
            f, s = first[t], second[t]
            r, l = up(s), down(s)
            lo, hi = pl.ds(0, 32), pl.ds(32, 32)
            arrived(k, t, 6, gs.at[k, t, f, l])
            start(k, t, 8, gs.at[k, t, f, l, lo], gs.at[k, t, f, l, lo], dev_second(t, r))
            arrived(k, t, 7, gs.at[k, t, f, r])
            start(k, t, 8, gs.at[k, t, f, r, hi], gs.at[k, t, f, r, hi], dev_second(t, l))

    def stage6(k):
        for t in range(2):
            f, s = first[t], second[t]
            arrived(k, t, 8, gs.at[k, t, f, opp(s)])
            start(k, t, 9, gs.at[k, t, f], gs.at[k, t, f], dev_first(t, up(f)))
            start(k, t, 10, gs.at[k, t, f], gs.at[k, t, f], dev_first(t, down(f)))

    def stage7(k):
        for t in range(2):
            f = first[t]
            r, l = up(f), down(f)
            lo, hi = pl.ds(0, 2), pl.ds(2, 2)
            arrived(k, t, 9, gs.at[k, t, l])
            start(k, t, 11, gs.at[k, t, l, lo], gs.at[k, t, l, lo], dev_first(t, r))
            arrived(k, t, 10, gs.at[k, t, r])
            start(k, t, 11, gs.at[k, t, r, hi], gs.at[k, t, r, hi], dev_first(t, l))

    def gw_copies(k):
        g = lax.rem(k, 2)
        return [
            pltpu.make_async_copy(
                gwst.at[g, r], gw_hbm.at[pl.ds(r * CBK + 2 * WB * k, 2 * WB)], gsem.at[g, r]
            )
            for r in range(RB)
        ]

    def arrive8(k):
        for t in range(2):
            f = first[t]
            arrived(k, t, 11, gs.at[k, t, opp(f)])
            sent(k, t, 2, gs.at[k, t, f, pl.ds(0, 3)])
            sent(k, t, 3, gs.at[k, t, pl.ds(0, 3)])

    def whole_g(k):
        g0 = jnp.concatenate([gs[k, 0, n // 4, n % 4] for n in range(16)], axis=0)
        g1 = jnp.concatenate([gs[k, 1, n % 4, n // 4] for n in range(16)], axis=0)
        return jnp.concatenate([g0, g1], axis=1)

    def slot_grads(k, g):
        @pl.when(k >= 2)
        def _():
            for d in gw_copies(k - 2):
                d.wait()

        wg = jnp.dot(xt[...], g, preferred_element_type=F32).astype(BF16)
        for r in range(RB):
            for j in range(2 * WB):
                gwst[lax.rem(k, 2), r, j] = wg[r * BLK:(r + 1) * BLK, j * BLK:(j + 1) * BLK]
        for d in gw_copies(k):
            d.start()

    def stage8(k):
        arrive8(k)
        g = whole_g(k)
        term = lax.dot_general(
            g, weights(k), (((1,), (1,)), ((), ())), preferred_element_type=F32
        )
        dxa[...] += term.reshape(8, BLK, RB * BLK)
        slot_grads(k, g)

    stages = (stage0, stage1, stage2, stage3, stage4, stage5, stage6, stage7, stage8)

    def early(j):
        for k in range(EARLY):
            rows(k, j, weights(k))
            o = opp(xr)

            @pl.when(o == j)
            def _():
                push(k, 0, 0)
                push(k, 0, 1)

            @pl.when(up(xr) == j)
            def _():
                push(k, 0, 2)

            @pl.when(down(xr) == j)
            def _():
                push(k, 0, 3)

            if j == 0:
                push(k, 1, 0)
                push(k, 1, 3)
            if j == 3:
                push(k, 1, 1)
                push(k, 1, 2)

    for n in range(2):
        got(n, xq(0, c, n))
        go(0, 9 + n, xq(0, c, n), xq(3, c, n), zr_dev)
        got(6 + n, xq(2, c, n + 2))
        go(0, 11 + n, xq(2, c, n + 2), xq(3, c, n + 2), zl_dev)
        go(0, 13, xq(0, c, n), xq(0, c, n), sib)
        go(0, 14, xq(2, c, n + 2), xq(2, c, n + 2), sib)
    for n in range(2):
        got(2 + n, xq(0, c, n + 2))
        go(0, 13, xq(0, c, n + 2), xq(0, c, n + 2), sib)
        got(4 + n, xq(2, c, n))
        go(0, 14, xq(2, c, n), xq(2, c, n), sib)
    early(1)
    for n in range(2):
        got(9 + n, xq(3, c, n))
        go(0, 15, xq(3, c, n), xq(3, c, n), sib)
        got(11 + n, xq(3, c, n + 2))
        go(0, 15, xq(3, c, n + 2), xq(3, c, n + 2), sib)
    got(13, xs.at[1 - c])
    early(0)
    got(14, xs.at[4 + 1 - c])
    early(2)
    got(15, xs.at[6 + 1 - c])
    early(3)
    ac(0, 0, xs.at[pl.ds(0, 7)], xs.at[pl.ds(0, 7)], sib).wait_send()
    gcopy.wait()

    def body(i, carry):
        @pl.when(i == 2)
        def _():
            for r in range(RB):
                for q in range(8):
                    xt[r * BLK:(r + 1) * BLK, q * BLK:(q + 1) * BLK] = xs[q, :, r * BLK:(r + 1) * BLK].T

        for n in range(len(stages) - 1, -1, -1):
            k = i - n

            @pl.when((k >= (0 if n else EARLY)) & (k < NCH))
            def _():
                stages[n](k)

        return carry

    lax.fori_loop(1, NCH + len(stages) - 2, body, 0)

    last = NCH - 1
    arrive8(last)
    rhs = weights(last)
    for q in (3, 2, 0, 1):
        g0 = jnp.concatenate([gs[last, 0, q, m] for m in range(4)], axis=0)
        g1 = jnp.concatenate([gs[last, 1, m, q] for m in range(4)], axis=0)
        g = jnp.concatenate([g0, g1], axis=1)
        term = lax.dot_general(g, rhs, (((1,), (1,)), ((), ())), preferred_element_type=F32)
        dxa[2 * q:2 * q + 2] += term.reshape(2, BLK, RB * BLK)
        sb[q] = dxa[2 * q + (1 - c)].astype(BF16)
        go(1, 16 + q, sb.at[q], sr.at[q], sib)
    lo, hi = pl.ds(0, 64), pl.ds(64, 64)

    def join(q):
        got(16 + q, sr.at[q])
        eb[q] = (dxa[2 * q + c] + sr[q].astype(F32)).astype(BF16)

    join(3)
    go(1, 20, eb.at[3, lo], u1.at[0], zr_dev)
    go(1, 21, eb.at[3, hi], u1.at[1], zl_dev)
    join(2)
    go(1, 22, eb.at[2, hi], u2.at[0, hi], zr_dev)
    join(0)
    go(1, 22, eb.at[0, lo], u2.at[1, lo], zl_dev)
    join(1)
    got(20, u1.at[0])
    eb[2, lo] = add2(eb[2, lo], u1[0])
    go(1, 22, eb.at[2, lo], u2.at[0, lo], zr_dev)
    got(21, u1.at[1])
    eb[0, hi] = add2(eb[0, hi], u1[1])
    go(1, 22, eb.at[0, hi], u2.at[1, hi], zl_dev)
    slot_grads(last, whole_g(last))
    for k in range(NCH - SL, NCH):
        for t in range(2):
            cols = pl.ds((2 * k + t) * W, W)
            pltpu.make_async_copy(
                act.at[k % SL, t], act_hbm.at[:, cols], osem.at[k % SL, t]
            ).wait()
    for k in (last - 1, last):
        for d in gw_copies(k):
            d.wait()
    got(22, u2)
    dx_out[...] = eb[1].astype(F32) + u2[0].astype(F32) + u2[1].astype(F32)
    ac(1, 0, xs.at[pl.ds(0, 7)], xs.at[pl.ds(0, 7)], sib).wait_send()


def pick_kernel(rows, cols, count, act_in, dx_in, gwd, act, dx, gw, abuf, dbuf, gbuf, obuf, sem, gsem, osem):
    row0 = lax.axis_index("inb") * RB
    col0 = lax.axis_index("outb") * CBK

    def fetch(s):
        cell = (rows[s] - row0) * CBK + cols[s] - col0
        return pltpu.make_async_copy(gwd.at[cell], gbuf.at[s], gsem.at[s // 8])

    def begin(s, carry):
        fetch(s).start()
        return carry

    lax.fori_loop(0, CAP, begin, 0, unroll=4)
    ins = [
        pltpu.make_async_copy(act_in, abuf, sem.at[0]),
        pltpu.make_async_copy(dx_in, dbuf, sem.at[1]),
    ]
    for d in ins:
        d.start()
    outs = [
        pltpu.make_async_copy(abuf, act, sem.at[2]),
        pltpu.make_async_copy(dbuf, dx, sem.at[3]),
    ]

    def flush(n):
        return pltpu.make_async_copy(
            obuf.at[pl.ds(n * 8, 8)], gw.at[pl.ds(n * 8, 8)], osem.at[n]
        )

    def group(n, carry):
        group8 = pl.ds(n * 8, 8)
        pltpu.make_async_copy(gwd.at[group8], gbuf.at[group8], gsem.at[n]).wait()
        for m in range(8):
            s = n * 8 + m
            alive = (s < count[0, 0]).astype(F32)
            obuf[s] = gbuf[s].astype(F32) * alive
        flush(n).start()
        return carry

    lax.fori_loop(0, CAP // 8, group, 0)
    for d, e in zip(ins, outs):
        d.wait()
        e.start()

    def done(n, carry):
        flush(n).wait()
        return carry

    lax.fori_loop(0, CAP // 8, done, 0)
    for e in outs:
        e.wait()


def per_device(tokens, weight_blocks, block_rows, block_cols, block_count, grad_act):
    vmem = pl.BlockSpec(memory_space=pltpu.VMEM)
    smem = pl.BlockSpec(memory_space=pltpu.SMEM)
    hbm = pl.BlockSpec(memory_space=pl.ANY)
    rows, cols, count = block_rows[0, 0], block_cols[0, 0], block_count
    act_shape = jax.ShapeDtypeStruct((64, CBK * BLK), BF16)
    dx_shape = jax.ShapeDtypeStruct((BLK, RB * BLK), F32)
    act, dx, gwd = pl.pallas_call(
        kernel,
        out_shape=(
            act_shape,
            dx_shape,
            jax.ShapeDtypeStruct((RB * CBK, BLK, BLK), BF16),
        ),
        in_specs=[smem, smem, smem, hbm, hbm, hbm],
        out_specs=(hbm, vmem, hbm),
        scratch_shapes=[
            pltpu.SMEM((8, BLK), jnp.int32),
            pltpu.VMEM((8, BLK), jnp.int32),
            pltpu.VMEM((CAP + 1, BLK, BLK), BF16),
            pltpu.VMEM((8, BLK, RB * BLK), BF16),
            pltpu.VMEM((RB * BLK, 1024), BF16),
            pltpu.VMEM((SL, 2, 4, 4, 64, W), BF16),
            pltpu.VMEM((SL, 2, 2, 2, 64, W), BF16),
            pltpu.VMEM((SL, 2, 2, 4, 64, W), BF16),
            pltpu.VMEM((SL, 2, 4, 64, W), BF16),
            pltpu.VMEM((SL, 2, 2, 32, W), BF16),
            pltpu.VMEM((SL, 2, 2, 64, W), BF16),
            pltpu.VMEM((NCH, 2, 4, 4, 64, W), BF16),
            pltpu.VMEM((8, BLK, RB * BLK), F32),
            pltpu.VMEM((64, CBK * BLK), BF16),
            pltpu.VMEM((SL, 2, 64, W), BF16),
            pltpu.VMEM((2, RB, 2 * WB, BLK, BLK), BF16),
            pltpu.VMEM((4, BLK, RB * BLK), BF16),
            pltpu.VMEM((4, BLK, RB * BLK), BF16),
            pltpu.VMEM((4, BLK, RB * BLK), BF16),
            pltpu.VMEM((2, 64, RB * BLK), BF16),
            pltpu.VMEM((2, BLK, RB * BLK), BF16),
            pltpu.SemaphoreType.DMA((SL, 2, 4)),
            pltpu.SemaphoreType.DMA((SL, 2, 12)),
            pltpu.SemaphoreType.DMA((2,)),
            pltpu.SemaphoreType.DMA((23,)),
            pltpu.SemaphoreType.DMA((4,)),
            pltpu.SemaphoreType.DMA((SL, 2)),
            pltpu.SemaphoreType.DMA((2, RB)),
        ],
        compiler_params=pltpu.CompilerParams(
            collective_id=0, has_side_effects=True, vmem_limit_bytes=67043328
        ),
        name="ffn",
    )(rows, cols, count, tokens, weight_blocks[0, 0], grad_act)
    act, dx, gw = pl.pallas_call(
        pick_kernel,
        out_shape=(act_shape, dx_shape, jax.ShapeDtypeStruct((CAP, BLK, BLK), F32)),
        in_specs=[smem, smem, smem, hbm, hbm, hbm],
        out_specs=(hbm, hbm, hbm),
        scratch_shapes=[
            pltpu.VMEM(act_shape.shape, BF16),
            pltpu.VMEM(dx_shape.shape, F32),
            pltpu.VMEM((CAP, BLK, BLK), BF16),
            pltpu.VMEM((CAP, BLK, BLK), F32),
            pltpu.SemaphoreType.DMA((4,)),
            pltpu.SemaphoreType.DMA((CAP // 8,)),
            pltpu.SemaphoreType.DMA((CAP // 8,)),
        ],
        compiler_params=pltpu.CompilerParams(vmem_limit_bytes=67043328),
        name="pick",
    )(rows, cols, count, act, dx, gwd)
    return (act, dx, gw[None, None])


def solution(mesh):
    in_specs = (
        P("outb", "inb"),
        P("inb", "outb", None, None, None),
        P("inb", "outb", None),
        P("inb", "outb", None),
        P("inb", "outb"),
        P("inb", "outb"),
    )
    out_specs = (P("inb", "outb"), P("outb", "inb"), P("inb", "outb", None, None, None))
    return jax.shard_map(
        per_device, mesh=mesh, in_specs=in_specs, out_specs=out_specs, check_vma=False
    )
```

time: 174 us -> 173 us (level)
  Pallas kernels: 173 us -> 171 us
where the time goes in v4:
time: 173 us; the launch traced here: 172 us
  Pallas kernels  171 us (99%)
    pallas_call x1, Pallas kernels, per_device(): pl.pallas_call(kernel, out_shape=(act_shape, dx_shape, jax.ShapeDtypeStru...  167 us
    pallas_call x1, Pallas kernels, per_device(): pl.pallas_call(pick_kernel, out_shape=(act_shape, dx_shape, jax.ShapeDtyp...  4.34 us

profile of v4, /device:TPU:0, one launch (start us, length us, event | category | flops | bytes accessed | tf_op | source)
XLA Modules:
  0.0 172.3 jit_solution(9916239869625879061)
XLA Ops:
  1.3 166.7 %ffn.1 = (bf16[64,6144]{1,0:T(8,128)(2,1)}, f32[128,768]{1,0:T(8,128)}, bf16[288,128,128]{2,1,0:T(8,128)(2,1)}) custom-call(s32[72]{0:T(128)} %bitcast.5, s32[72]{0:T(128)} %bitcast.7, s32[1,1]{1,0:T(1,128)S(6)} %copy.9.count_in.count, bf16[128,768]{1,0:T(8,128)(2,1)} %tok.1, bf16[72,128,128]{2,1,0:T(8,128)(2,1)} %bitcast.4, bf16[64,6144]{1,0:T(8,128)(2,1)} %gact_hbm.1), custom_call_target="tpu_custom_call" | custom-call | tf_op jit(solution)/shard_map/ffn/pallas_call | solution.py:491
  167.9 4.3 %pick.1 = (bf16[64,6144]{1,0:T(8,128)(2,1)}, f32[128,768]{1,0:T(8,128)}, f32[72,128,128]{2,1,0:T(8,128)}) custom-call(s32[72]{0:T(128)} %bitcast.6, s32[72]{0:T(128)} %bitcast.8, s32[1,1]{1,0:T(1,128)S(6)} %copy.9.count_in.count, bf16[64,6144]{1,0:T(8,128)(2,1)} %get-tuple-element.9.act_in, f32[128,768]{1,0:T(8,128)} %get-tuple-element.10.dx_in, ...), custom_call_target="tpu_custom_call" | custom-call | tf_op jit(solution)/shard_map/pick/pallas_call | solution.py:535

commit v5 on v4

--- a/solution.py
+++ b/solution.py
@@ -110,13 +110,13 @@
     def xq(j, cc, h):
         return xs.at[2 * j + cc, pl.ds(32 * h, 32)]
 
+    xcopy.wait()
     for n in range(4):
         m = (n + 2) % 4
-        go(0, n, tok.at[pl.ds(32 * n, 32)], xq(0, c, n), zr_dev)
-        go(0, 4 + m, tok.at[pl.ds(32 * m, 32)], xq(2, c, m), zl_dev)
-    go(0, 8, tok, xs.at[2 + c], sib)
+        go(0, n, xq(1, c, n), xq(0, c, n), zr_dev)
+        go(0, 4 + m, xq(1, c, m), xq(2, c, m), zl_dev)
+    go(0, 8, xs.at[2 + c], xs.at[2 + c], sib)
     dxa[...] = jnp.zeros_like(dxa)
-    xcopy.wait()
     wcopy.wait()
     tcopy.wait()
     got(8, xs.at[2 + 1 - c])
@@ -203,8 +203,6 @@
             lo, hi = pl.ds(0, 32), pl.ds(32, 32)
             start(k, t, 3, qs.at[slot, t, o, lo], t1.at[slot, t, 0], dev_second(t, r))
             start(k, t, 4, qs.at[slot, t, o, hi], t1.at[slot, t, 1], dev_second(t, l))
-            start(k, t, 5, qs.at[slot, t, r, hi], t2.at[slot, t, 0, hi], dev_second(t, r))
-            start(k, t, 5, qs.at[slot, t, l, lo], t2.at[slot, t, 1, lo], dev_second(t, l))
 
     def stage3(k):
         slot = lax.rem(k, SL)
@@ -214,10 +212,10 @@
             lo, hi = pl.ds(0, 32), pl.ds(32, 32)
             arrived(k, t, 3, t1.at[slot, t, 0])
             qs[slot, t, r, lo] = add2(qs[slot, t, r, lo], t1[slot, t, 0])
-            start(k, t, 5, qs.at[slot, t, r, lo], t2.at[slot, t, 0, lo], dev_second(t, r))
+            start(k, t, 5, qs.at[slot, t, r], t2.at[slot, t, 0], dev_second(t, r))
             arrived(k, t, 4, t1.at[slot, t, 1])
             qs[slot, t, l, hi] = add2(qs[slot, t, l, hi], t1[slot, t, 1])
-            start(k, t, 5, qs.at[slot, t, l, hi], t2.at[slot, t, 1, hi], dev_second(t, l))
+            start(k, t, 5, qs.at[slot, t, l], t2.at[slot, t, 1], dev_second(t, l))
 
     def stage4(k):
         slot = lax.rem(k, SL)
@@ -262,6 +260,7 @@
             f = first[t]
             r, l = up(f), down(f)
             lo, hi = pl.ds(0, 2), pl.ds(2, 2)
+            sent(k, t, 2, gs.at[k, t, f, pl.ds(0, 3)])
             arrived(k, t, 9, gs.at[k, t, l])
             start(k, t, 11, gs.at[k, t, l, lo], gs.at[k, t, l, lo], dev_first(t, r))
             arrived(k, t, 10, gs.at[k, t, r])
@@ -280,7 +279,6 @@
         for t in range(2):
             f = first[t]
             arrived(k, t, 11, gs.at[k, t, opp(f)])
-            sent(k, t, 2, gs.at[k, t, f, pl.ds(0, 3)])
             sent(k, t, 3, gs.at[k, t, pl.ds(0, 3)])
 
     def whole_g(k):
@@ -371,7 +369,7 @@
                 for q in range(8):
                     xt[r * BLK:(r + 1) * BLK, q * BLK:(q + 1) * BLK] = xs[q, :, r * BLK:(r + 1) * BLK].T
 
-        for n in range(len(stages) - 1, -1, -1):
+        for n in (7, 6, 5, 4, 3, 2, 1, 0, 8):
             k = i - n
 
             @pl.when((k >= (0 if n else EARLY)) & (k < NCH))

time: 173 us -> 171 us (0.988)
  Pallas kernels: 171 us -> 169 us
where the time goes in v5:
time: 171 us
  Pallas kernels  169 us (99%)
    pallas_call x1, Pallas kernels, per_device(): pl.pallas_call(kernel, out_shape=(act_shape, dx_shape, jax.ShapeDtypeStru...  165 us
    pallas_call x1, Pallas kernels, per_device(): pl.pallas_call(pick_kernel, out_shape=(act_shape, dx_shape, jax.ShapeDtyp...  4.34 us

profile of v5, /device:TPU:0, one launch (start us, length us, event | category | flops | bytes accessed | tf_op | source)
XLA Modules:
  0.0 170.6 jit_solution(151742308196810703)
XLA Ops:
  1.3 165.0 %ffn.1 = (bf16[64,6144]{1,0:T(8,128)(2,1)}, f32[128,768]{1,0:T(8,128)}, bf16[288,128,128]{2,1,0:T(8,128)(2,1)}) custom-call(s32[72]{0:T(128)} %bitcast.5, s32[72]{0:T(128)} %bitcast.7, s32[1,1]{1,0:T(1,128)S(6)} %copy.9.count_in.count, bf16[128,768]{1,0:T(8,128)(2,1)} %tok.1, bf16[72,128,128]{2,1,0:T(8,128)(2,1)} %bitcast.4, bf16[64,6144]{1,0:T(8,128)(2,1)} %gact_hbm.1), custom_call_target="tpu_custom_call" | custom-call | tf_op jit(solution)/shard_map/ffn/pallas_call | solution.py:489
  166.3 4.3 %pick.1 = (bf16[64,6144]{1,0:T(8,128)(2,1)}, f32[128,768]{1,0:T(8,128)}, f32[72,128,128]{2,1,0:T(8,128)}) custom-call(s32[72]{0:T(128)} %bitcast.6, s32[72]{0:T(128)} %bitcast.8, s32[1,1]{1,0:T(1,128)S(6)} %copy.9.count_in.count, bf16[64,6144]{1,0:T(8,128)(2,1)} %get-tuple-element.9.act_in, f32[128,768]{1,0:T(8,128)} %get-tuple-element.10.dx_in, ...), custom_call_target="tpu_custom_call" | custom-call | tf_op jit(solution)/shard_map/pick/pallas_call | solution.py:533

commit v6 on v5

--- a/solution.py
+++ b/solution.py
@@ -158,24 +158,16 @@
             rows(lax.rem(k, SL), m, rhs)
         send0(k)
 
-    def push(k, t, n):
+    def send0(k):
         slot = lax.rem(k, SL)
-        f = first[t]
-        r, l, o = up(f), down(f), opp(f)
-        lo, hi = pl.ds(0, 2), pl.ds(2, 2)
-        if n == 0:
+        for t in range(2):
+            f = first[t]
+            r, l, o = up(f), down(f), opp(f)
+            lo, hi = pl.ds(0, 2), pl.ds(2, 2)
             start(k, t, 0, ps.at[slot, t, o, lo], r1.at[slot, t, 0], dev_first(t, r))
-        elif n == 1:
             start(k, t, 1, ps.at[slot, t, o, hi], r1.at[slot, t, 1], dev_first(t, l))
-        elif n == 2:
             start(k, t, 2, ps.at[slot, t, r, hi], r2.at[slot, t, 0, hi], dev_first(t, r))
-        else:
             start(k, t, 2, ps.at[slot, t, l, lo], r2.at[slot, t, 1, lo], dev_first(t, l))
-
-    def send0(k):
-        for t in range(2):
-            for n in range(4):
-                push(k, t, n)
 
     def stage1(k):
         slot = lax.rem(k, SL)
@@ -313,27 +305,6 @@
     def early(j):
         for k in range(EARLY):
             rows(k, j, weights(k))
-            o = opp(xr)
-
-            @pl.when(o == j)
-            def _():
-                push(k, 0, 0)
-                push(k, 0, 1)
-
-            @pl.when(up(xr) == j)
-            def _():
-                push(k, 0, 2)
-
-            @pl.when(down(xr) == j)
-            def _():
-                push(k, 0, 3)
-
-            if j == 0:
-                push(k, 1, 0)
-                push(k, 1, 3)
-            if j == 3:
-                push(k, 1, 1)
-                push(k, 1, 2)
 
     for n in range(2):
         got(n, xq(0, c, n))
@@ -359,6 +330,8 @@
     early(2)
     got(15, xs.at[6 + 1 - c])
     early(3)
+    for k in range(EARLY):
+        send0(k)
     ac(0, 0, xs.at[pl.ds(0, 7)], xs.at[pl.ds(0, 7)], sib).wait_send()
     gcopy.wait()
 

time: 171 us -> 170 us (level)
  no operation moved by 1% of the time
where the time goes in v6:
time: 170 us; the launch traced here: 169 us
  Pallas kernels  168 us (99%)
    pallas_call x1, Pallas kernels, per_device(): pl.pallas_call(kernel, out_shape=(act_shape, dx_shape, jax.ShapeDtypeStru...  164 us
    pallas_call x1, Pallas kernels, per_device(): pl.pallas_call(pick_kernel, out_shape=(act_shape, dx_shape, jax.ShapeDtyp...  4.34 us

profile of v6, /device:TPU:0, one launch (start us, length us, event | category | flops | bytes accessed | tf_op | source)
XLA Modules:
  0.0 169.5 jit_solution(14408385991393966713)
XLA Ops:
  1.3 163.8 %ffn.1 = (bf16[64,6144]{1,0:T(8,128)(2,1)}, f32[128,768]{1,0:T(8,128)}, bf16[288,128,128]{2,1,0:T(8,128)(2,1)}) custom-call(s32[72]{0:T(128)} %bitcast.5, s32[72]{0:T(128)} %bitcast.7, s32[1,1]{1,0:T(1,128)S(6)} %copy.9.count_in.count, bf16[128,768]{1,0:T(8,128)(2,1)} %tok.1, bf16[72,128,128]{2,1,0:T(8,128)(2,1)} %bitcast.4, bf16[64,6144]{1,0:T(8,128)(2,1)} %gact_hbm.1), custom_call_target="tpu_custom_call" | custom-call | tf_op jit(solution)/shard_map/ffn/pallas_call | solution.py:462
  165.1 4.3 %pick.1 = (bf16[64,6144]{1,0:T(8,128)(2,1)}, f32[128,768]{1,0:T(8,128)}, f32[72,128,128]{2,1,0:T(8,128)}) custom-call(s32[72]{0:T(128)} %bitcast.6, s32[72]{0:T(128)} %bitcast.8, s32[1,1]{1,0:T(1,128)S(6)} %copy.9.count_in.count, bf16[64,6144]{1,0:T(8,128)(2,1)} %get-tuple-element.9.act_in, f32[128,768]{1,0:T(8,128)} %get-tuple-element.10.dx_in, ...), custom_call_target="tpu_custom_call" | custom-call | tf_op jit(solution)/shard_map/pick/pallas_call | solution.py:506

commit v7 on v6

--- a/solution.py
+++ b/solution.py
@@ -336,18 +336,18 @@
     gcopy.wait()
 
     def body(i, carry):
-        @pl.when(i == 2)
+        for n in (7, 6, 5, 4, 3, 2, 1, 0, 8):
+            k = i - n
+
+            @pl.when((k >= (0 if n else EARLY)) & (k < NCH))
+            def _():
+                stages[n](k)
+
+        @pl.when(i == 6)
         def _():
             for r in range(RB):
                 for q in range(8):
                     xt[r * BLK:(r + 1) * BLK, q * BLK:(q + 1) * BLK] = xs[q, :, r * BLK:(r + 1) * BLK].T
-
-        for n in (7, 6, 5, 4, 3, 2, 1, 0, 8):
-            k = i - n
-
-            @pl.when((k >= (0 if n else EARLY)) & (k < NCH))
-            def _():
-                stages[n](k)
 
         return carry
 

time: 170 us -> 170 us (level)
  no operation moved by 1% of the time
where the time goes in v7:
time: 170 us; the launch traced here: 169 us
  Pallas kernels  168 us (99%)
    pallas_call x1, Pallas kernels, per_device(): pl.pallas_call(kernel, out_shape=(act_shape, dx_shape, jax.ShapeDtypeStru...  164 us
    pallas_call x1, Pallas kernels, per_device(): pl.pallas_call(pick_kernel, out_shape=(act_shape, dx_shape, jax.ShapeDtyp...  4.34 us

profile of v7, /device:TPU:0, one launch (start us, length us, event | category | flops | bytes accessed | tf_op | source)
XLA Modules:
  0.0 169.5 jit_solution(7248434324888459584)
XLA Ops:
  1.3 163.8 %ffn.1 = (bf16[64,6144]{1,0:T(8,128)(2,1)}, f32[128,768]{1,0:T(8,128)}, bf16[288,128,128]{2,1,0:T(8,128)(2,1)}) custom-call(s32[72]{0:T(128)} %bitcast.5, s32[72]{0:T(128)} %bitcast.7, s32[1,1]{1,0:T(1,128)S(6)} %copy.9.count_in.count, bf16[128,768]{1,0:T(8,128)(2,1)} %tok.1, bf16[72,128,128]{2,1,0:T(8,128)(2,1)} %bitcast.4, bf16[64,6144]{1,0:T(8,128)(2,1)} %gact_hbm.1), custom_call_target="tpu_custom_call" | custom-call | tf_op jit(solution)/shard_map/ffn/pallas_call | solution.py:462
  165.1 4.3 %pick.1 = (bf16[64,6144]{1,0:T(8,128)(2,1)}, f32[128,768]{1,0:T(8,128)}, f32[72,128,128]{2,1,0:T(8,128)}) custom-call(s32[72]{0:T(128)} %bitcast.6, s32[72]{0:T(128)} %bitcast.8, s32[1,1]{1,0:T(1,128)S(6)} %copy.9.count_in.count, bf16[64,6144]{1,0:T(8,128)(2,1)} %get-tuple-element.9.act_in, f32[128,768]{1,0:T(8,128)} %get-tuple-element.10.dx_in, ...), custom_call_target="tpu_custom_call" | custom-call | tf_op jit(solution)/shard_map/pick/pallas_call | solution.py:506
